TPU v7x, 32 devices: a whole 2x2x4 slice. The times are simulated.
32 devices in a mesh: groups: 2 (over x), ctx: 16 (over z, y, core).
Axes of the slice: x: 2, y: 2, z: 4, core: 2. Of those that a mesh axis runs over, the one named last changes fastest.
Arguments:
- value_stream: bfloat16 [4096, 2048], P(('groups', 'ctx')), parts along dimension 0, may hold values from -6 to 6
- gate_stream: bfloat16 [4096, 2048], P(('groups', 'ctx')), parts along dimension 0, may hold values from -6 to 6
- filter_spectrum: bfloat16 [2, 2, 2048, 2048], P(None, None, 'ctx'), may hold values from -6 to 6
- router: bfloat16 [2048, 16], replicated, may hold values from -0.125 to 0.125
- w_gate: bfloat16 [2048, 45056], P(None, 'ctx'), may hold values from -0.125 to 0.125
- w_up: bfloat16 [2048, 45056], P(None, 'ctx'), may hold values from -0.125 to 0.125
- w_down: bfloat16 [45056, 2048], P('ctx'), may hold values from -0.109375 to 0.109375
- route_ids: int32 [2, 4096], P(None, ('groups', 'ctx')), parts along dimension 1, may hold values from 0 to 15, as said below
- route_slots: int32 [2, 4096], P(None, ('groups', 'ctx')), parts along dimension 1, may hold values from 0 to 20, as said below
Outputs:
- layer_out: bfloat16 [4096, 2048], P(('groups', 'ctx')), parts along dimension 0
There are 2 independent parts, one for each index of `groups`. A program takes and returns all parts, laid end to end along the dimension named above; an argument that names none is the same for every part. Nothing has to cross between parts.
Inputs may be any that keep to these rules, and one draw needn't show every extreme that they name: `route_ids`: each token names 2 different experts. route_slots[k, r] is the number of earlier choices of the same expert among the tokens of r's ctx index, tokens taken in order and a token's choices in order k = 0, 1, clipped to 20; so at most 20 choices of one expert from one ctx index are kept, and in every draw some expert has its 20 slots filled from every ctx index.
All inputs are finite; a program needn't handle non-finite values.
Results may differ from a plain program's by a relative error of at most 0.0058.
Values may be sent and summed in bfloat16 or wider, within the bound.
A program may use at most 128 MiB of HBM per device.

v0:
```python
import jax
import jax.numpy as jnp
import numpy as np
from jax import lax
from jax.sharding import PartitionSpec as P

CAP = 20


two_pi = 2.0 * np.pi
highest = lax.Precision.HIGHEST


def reverse_bits(length_n):
    bit_count = length_n.bit_length() - 1
    positions = np.arange(length_n)
    reversed_index = np.zeros(length_n, dtype=np.int64)
    for position in range(bit_count):
        reversed_index = reversed_index | (positions >> position & 1) << bit_count - 1 - position
    return reversed_index


def dft_table(length_n):
    exponent = np.outer(reverse_bits(length_n), np.arange(length_n)) % length_n
    angle_rad = -two_pi * exponent / length_n
    return (
        jnp.asarray(np.cos(angle_rad), jnp.float32),
        jnp.asarray(np.sin(angle_rad), jnp.float32),
    )


def rotation(numerator, denominator):
    angle_rad = -two_pi * (numerator.astype(jnp.float32) / denominator)
    return (jnp.cos(angle_rad), jnp.sin(angle_rad))


def complex_times(stacked, real_factor, imag_factor):
    real_part = stacked[0] * real_factor - stacked[1] * imag_factor
    imag_part = stacked[0] * imag_factor + stacked[1] * real_factor
    return jnp.stack([real_part, imag_part])


def mix_form(table_re, table_im, stacked, form):
    real_part = jnp.einsum(form, table_re, stacked[0], precision=highest) - jnp.einsum(
        form, table_im, stacked[1], precision=highest
    )
    imag_part = jnp.einsum(form, table_re, stacked[1], precision=highest) + jnp.einsum(
        form, table_im, stacked[0], precision=highest
    )
    return jnp.stack([real_part, imag_part])


def mix_rows(table_re, table_im, stacked):
    return mix_form(table_re, table_im, stacked, "oi,bi...->bo...")


def local(
    value_stream, gate_stream, filter_spectrum, router, w_gate, w_up, w_down, route_ids, route_slots
):
    tok_rows, channels = value_stream.shape
    size_ctx = lax.axis_size("ctx")
    device = lax.axis_index("ctx")
    seq_len = tok_rows * size_ctx
    tok_re, tok_im = dft_table(tok_rows)
    ctx_re, ctx_im = dft_table(size_ctx)
    ctx_order = jnp.asarray(reverse_bits(size_ctx), jnp.int32)
    slice_rows = tok_rows // size_ctx
    column_pos = device * slice_rows + jnp.arange(slice_rows, dtype=jnp.int32)
    twist_cos, twist_sin = rotation(ctx_order[:, None] * column_pos[None, :] % seq_len, seq_len)
    twist_cos = twist_cos[None, :, :, None]
    twist_sin = twist_sin[None, :, :, None]
    arrived = lax.all_to_all(
        value_stream.reshape(1, tok_rows, channels), "ctx", split_axis=1, concat_axis=0, tiled=True
    )
    source_pos = jnp.arange(size_ctx, dtype=jnp.int32)[:, None] * tok_rows + column_pos[None, :]
    spread_cos, spread_sin = rotation(source_pos, 2 * seq_len)
    spread_cos = spread_cos[:, :, None]
    spread_sin = spread_sin[:, :, None]
    samples = arrived.astype(jnp.float32)
    zeros_part = jnp.zeros_like(samples)
    spread = jnp.stack(
        [jnp.stack([samples, samples * spread_cos]), jnp.stack([zeros_part, samples * spread_sin])]
    )
    spread = mix_rows(ctx_re, ctx_im, spread)
    spread = complex_times(spread, twist_cos, twist_sin)
    spread = lax.all_to_all(spread, "ctx", split_axis=2, concat_axis=3, tiled=True)
    signal = spread.reshape(2, 2, tok_rows, channels)
    signal = mix_rows(tok_re, tok_im, signal)
    filter_local = filter_spectrum.astype(jnp.float32)
    signal = complex_times(signal, filter_local[0], filter_local[1])
    signal = mix_rows(tok_re.T, -tok_im.T, signal)
    spread = lax.all_to_all(
        signal.reshape(2, 2, 1, tok_rows, channels), "ctx", split_axis=3, concat_axis=2, tiled=True
    )
    spread = complex_times(spread, twist_cos, -twist_sin)
    spread = mix_rows(ctx_re.T, -ctx_im.T, spread)
    folded = (spread[0, 0] + spread_cos * spread[0, 1] + spread_sin * spread[1, 1]) / (2 * seq_len)
    long_conv = lax.all_to_all(folded, "ctx", split_axis=0, concat_axis=1, tiled=True).reshape(
        tok_rows, channels
    )
    hyena_out = (gate_stream.astype(jnp.float32) * long_conv).astype(jnp.bfloat16)
    hyena32 = hyena_out.astype(jnp.float32)
    inv_rms = lax.rsqrt(jnp.mean(hyena32 * hyena32, axis=1, keepdims=True) + 1e-06)
    normed = (hyena32 * inv_rms).astype(jnp.bfloat16)
    logits = jnp.dot(normed, router, preferred_element_type=jnp.float32)
    expert_count = router.shape[1]
    owner_split = size_ctx // expert_count
    slot_count = expert_count * CAP
    positions = jnp.arange(slot_count, dtype=jnp.int32)
    expert_range = jnp.arange(expert_count, dtype=jnp.int32)
    combine = jnp.zeros((tok_rows, slot_count), jnp.float32)
    dispatch = jnp.zeros((slot_count, channels), jnp.float32)
    for pick_index in range(route_ids.shape[0]):
        expert_ids = route_ids[pick_index]
        slot_ids = route_slots[pick_index]
        target = jnp.where(slot_ids < CAP, expert_ids * CAP + slot_ids, -1)
        slot_hits = target[:, None] == positions[None, :]
        chosen_logit = jnp.sum(
            jnp.where(expert_ids[:, None] == expert_range[None, :], logits, 0.0), axis=1
        )
        gate_value = jax.nn.sigmoid(chosen_logit)
        combine = combine + slot_hits.astype(jnp.float32) * gate_value[:, None]
        dispatch = dispatch + lax.dot_general(
            slot_hits.astype(jnp.bfloat16),
            normed,
            (((0,), (0,)), ((), ())),
            preferred_element_type=jnp.float32,
        )
    buffer = dispatch.astype(jnp.bfloat16).reshape(expert_count, CAP, channels)
    outgoing = jnp.repeat(buffer, owner_split, axis=0)
    slot_rows = lax.all_to_all(outgoing, "ctx", split_axis=0, concat_axis=0, tiled=True)
    flat_rows = slot_rows.reshape(-1, channels)
    gate_part = jnp.dot(flat_rows, w_gate, preferred_element_type=jnp.float32)
    up_part = jnp.dot(flat_rows, w_up, preferred_element_type=jnp.float32)
    hidden = (jax.nn.silu(gate_part) * up_part).astype(jnp.bfloat16)
    partial_value = jnp.dot(hidden, w_down, preferred_element_type=jnp.float32).astype(jnp.bfloat16)
    returned = lax.all_to_all(
        partial_value.reshape(slot_rows.shape), "ctx", split_axis=0, concat_axis=0, tiled=True
    )
    expert_out = jnp.sum(
        returned.astype(jnp.float32).reshape(expert_count, owner_split, CAP, channels), axis=1
    ).reshape(slot_count, channels)
    contribution = jnp.dot(combine, expert_out, precision=highest)
    return (hyena32 + contribution).astype(jnp.bfloat16)


def solution(mesh):
    in_specs = (
        P(("groups", "ctx"), None),
        P(("groups", "ctx"), None),
        P(None, None, "ctx", None),
        P(),
        P(None, "ctx"),
        P(None, "ctx"),
        P("ctx", None),
        P(None, ("groups", "ctx")),
        P(None, ("groups", "ctx")),
    )
    out_specs = P(("groups", "ctx"), None)
    return jax.shard_map(local, mesh=mesh, in_specs=in_specs, out_specs=out_specs, check_vma=False)
```

profile of v0, /device:TPU:0, one launch (start us, length us, event | category | flops | bytes accessed | tf_op | source)
XLA Modules:
  0.0 439.8 jit_solution(16760699648697569223)
XLA Ops:
  2.4 3.7 reduce
  7.5 7.4 %all-to-all-start = ((bf16[16,2,8192]{2,1,0:T(2,128)(2,1)}), bf16[16,2,8192]{2,1,0:T(2,128)(2,1)S(1)}, u32[]{:S(2)}, u32[]{:S(2)}) async-start(bf16[16,2,8192]{2,1,0:T(2,128)(2,1)} %reshape.305), calls=%async_computation | async-start | bytes 1048576 | tf_op jit(solution)/shard_map/all_to_all | solution.py:72
  15.0 14.3 %all-to-all-done = bf16[16,2,8192]{2,1,0:T(2,128)(2,1)S(1)} async-done(((bf16[16,2,8192]{2,1,0:T(2,128)(2,1)}), bf16[16,2,8192]{2,1,0:T(2,128)(2,1)S(1)}, u32[]{:S(2)}, u32[]{:S(2)}) %all-to-all-start) | async-done | bytes 524320 | tf_op jit(solution)/shard_map/all_to_all | solution.py:72
  35.0 2.0 fusion.7
  37.1 2.9 subtract_bitcast_fusion
  40.4 4.6 %copy.64 = f32[2,2,16,8,2048]{4,3,1,0,2:T(8,128)} copy(f32[2,2,16,8,2048]{4,2,3,1,0:T(8,128)S(1)} %pad_maximum_fusion) | data formatting | bytes 8388608 | tf_op jit(solution)/shard_map/stack | solution.py:40
  45.1 4.5 %all-to-all-start.1 = ((f32[2,2,16,8,2048]{4,3,1,0,2:T(8,128)}), f32[2,2,16,8,2048]{4,3,1,0,2:T(8,128)}, u32[]{:S(2)}, u32[]{:S(2)}) async-start(f32[2,2,16,8,2048]{4,3,1,0,2:T(8,128)} %copy.64), calls=%async_computation.1 | async-start | bytes 8388608 | tf_op jit(solution)/shard_map/all_to_all | solution.py:86
  49.6 3.0 copy.69
  52.7 2.2 convert_element_type.81
  54.9 72.3 %all-to-all-done.1 = f32[2,2,16,8,2048]{4,3,1,0,2:T(8,128)} async-done(((f32[2,2,16,8,2048]{4,3,1,0,2:T(8,128)}), f32[2,2,16,8,2048]{4,3,1,0,2:T(8,128)}, u32[]{:S(2)}, u32[]{:S(2)}) %all-to-all-start.1) | async-done | bytes 4194336 | tf_op jit(solution)/shard_map/all_to_all | solution.py:86
  127.2 2.5 fusion.60
  129.7 3.5 fusion.11
  133.2 3.4 fusion.12
  136.7 3.5 fusion.6
  140.2 4.0 multiply_subtract_fusion.1
  151.5 2.2 maximum_bitcast_fusion
  153.7 7.3 %copy.72 = f32[2,2,1,128,2048]{4,1,0,2,3:T(2,128)} copy(f32[2,2,1,128,2048]{3,4,1,0,2:T(8,128)} %maximum_bitcast_fusion) | data formatting | bytes 8388608 | tf_op jit(solution)/shard_map/reshape | solution.py:93
  161.1 111.9 %all_to_all.46 = f32[2,2,1,128,2048]{4,1,0,2,3:T(2,128)S(1)} all-to-all(f32[2,2,1,128,2048]{4,1,0,2,3:T(2,128)} %copy.72), channel_id=1, replica_groups=mesh['groups'=2,'ctx'=16] {'ctx'}, dimensions={3} | all-to-all | bytes 8388608 | tf_op jit(solution)/shard_map/all_to_all | solution.py:92
  272.9 2.3 fusion.59
  275.3 2.4 copy_bitcast_fusion
  277.7 4.7 %fusion.27 = f32[2,8,2048,16]{2,3,1,0:T(8,128)S(1)} fusion(f32[16,16,1,1]{1,0,3,2:T(8,128)S(1)} %copy-done.6, f32[2,16,8,2048]{3,2,1,0:T(8,128)S(1)} %get-tuple-element.30, f32[2,16,8,2048]{3,2,1,0:T(8,128)S(1)} %get-tuple-element.31, f32[16,8]{0,1:T(8,128)S(1)} %get-tuple-element.23, f32[16,8]{0,1:T(8,128)S(1)} %get-tuple-element.25), kind=kOutput, calls=%fused_computation.62 | convolution fusion | flops 102236160 | bytes 6293504 | tf_op jit(solution)/shard_map/oi,bi...->bo.../dot_general | solution.py:44
  282.4 5.1 %fusion.28 = f32[2,8,2048,16]{2,3,1,0:T(8,128)S(1)} fusion(f32[16,16,1,1]{1,0,3,2:T(8,128)S(1)} %copy-done.6, f32[2,16,8,2048]{3,2,1,0:T(8,128)S(1)} %get-tuple-element.30, f32[2,16,8,2048]{3,2,1,0:T(8,128)S(1)} %get-tuple-element.31, f32[16,8]{0,1:T(8,128)S(1)} %get-tuple-element.23, f32[16,8]{0,1:T(8,128)S(1)} %get-tuple-element.25), kind=kOutput, calls=%fused_computation.63 | convolution fusion | flops 102236160 | bytes 6293504 | tf_op jit(solution)/shard_map/oi,bi...->bo.../dot_general | solution.py:47
  287.5 4.7 %fusion.2 = f32[1,2,16,8,2048]{4,2,3,1,0:T(8,128)S(1)} fusion(f32[2,8,2048,16]{2,3,1,0:T(8,128)S(1)} %fusion.27, f32[16,16,1,1]{0,1,3,2:T(8,128)S(1)} %copy-done.7, f32[2,16,8,2048]{3,2,1,0:T(8,128)S(1)} %get-tuple-element.30, f32[2,16,8,2048]{3,2,1,0:T(8,128)S(1)} %get-tuple-element.31, f32[16,8]{0,1:T(8,128)S(1)} %get-tuple-element.23, ...), kind=kOutput, calls=%fused_computation.8 | convolution fusion | flops 102760448 | bytes 8390656 | tf_op jit(solution)/shard_map/oi,bi...->bo.../dot_general | solution.py:44
  292.2 4.7 %fusion.1 = f32[1,2,16,8,2048]{4,2,3,1,0:T(8,128)S(1)} fusion(f32[2,8,2048,16]{2,3,1,0:T(8,128)S(1)} %fusion.28, f32[16,16,1,1]{0,1,3,2:T(8,128)S(1)} %copy-done.7, f32[2,16,8,2048]{3,2,1,0:T(8,128)S(1)} %get-tuple-element.30, f32[2,16,8,2048]{3,2,1,0:T(8,128)S(1)} %get-tuple-element.31, f32[16,8]{0,1:T(8,128)S(1)} %get-tuple-element.23, ...), kind=kOutput, calls=%fused_computation.6 | convolution fusion | flops 102760448 | bytes 8390656 | tf_op jit(solution)/shard_map/oi,bi...->bo.../dot_general | solution.py:47
  299.0 5.3 %all-to-all-start.3 = ((f32[16,8,2048]{2,1,0:T(8,128)}), f32[16,8,2048]{2,1,0:T(8,128)S(1)}, u32[]{:S(2)}, u32[]{:S(2)}) async-start(f32[16,8,2048]{2,1,0:T(8,128)} %copy.81), calls=%async_computation.3 | async-start | bytes 2097152 | tf_op jit(solution)/shard_map/all_to_all | solution.py:98
  304.4 22.9 %all-to-all-done.3 = f32[16,8,2048]{2,1,0:T(8,128)S(1)} async-done(((f32[16,8,2048]{2,1,0:T(8,128)}), f32[16,8,2048]{2,1,0:T(8,128)S(1)}, u32[]{:S(2)}, u32[]{:S(2)}) %all-to-all-start.3) | async-done | bytes 1048608 | tf_op jit(solution)/shard_map/all_to_all | solution.py:98
  329.1 42.9 %all_to_all.47 = bf16[16,20,2048]{2,1,0:T(8,128)(2,1)} all-to-all(bf16[16,20,2048]{2,1,0:T(8,128)(2,1)S(1)} %reshape_broadcast_in_dim_reshape.3), channel_id=1, replica_groups=mesh['groups'=2,'ctx'=16] {'ctx'}, dimensions={0} | all-to-all | bytes 2621440 | tf_op jit(solution)/shard_map/all_to_all | solution.py:131
  372.0 2.3 reshape.293
  374.3 8.5 %fusion.64 = f32[320,2816]{1,0:T(8,128)} fusion(bf16[320,2048]{1,0:T(8,128)(2,1)S(1)} %reshape.293, bf16[2048,2816]{1,0:T(8,128)(2,1)} %param.18), kind=kOutput, calls=%fused_computation.119 | convolution fusion | flops 3690987520 | bytes 16449536 | tf_op jit(solution)/shard_map/dot_general | solution.py:133
  382.8 16.3 %convolution_convert_fusion = bf16[320,2048]{1,0:T(8,128)(2,1)S(1)} fusion(bf16[2816,2048]{1,0:T(8,128)(2,1)} %param.20, bf16[320,2048]{1,0:T(8,128)(2,1)S(1)} %reshape.293, bf16[2048,2816]{1,0:T(8,128)(2,1)} %param.19, f32[320,2816]{1,0:T(8,128)} %fusion.64), kind=kOutput, calls=%fused_computation.22 | convolution fusion | flops 7388037120 | bytes 29294592 | tf_op jit(solution)/shard_map/dot_general | solution.py:136
  400.4 5.0 %all-to-all-start.5 = ((bf16[16,20,2048]{2,1,0:T(8,128)(2,1)}), bf16[16,20,2048]{2,1,0:T(8,128)(2,1)S(1)}, u32[]{:S(2)}, u32[]{:S(2)}) async-start(bf16[16,20,2048]{2,1,0:T(8,128)(2,1)} %reshape.294), calls=%async_computation.5 | async-start | bytes 3145728 | tf_op jit(solution)/shard_map/all_to_all | solution.py:137
  405.8 31.6 %all-to-all-done.5 = bf16[16,20,2048]{2,1,0:T(8,128)(2,1)S(1)} async-done(((bf16[16,20,2048]{2,1,0:T(8,128)(2,1)}), bf16[16,20,2048]{2,1,0:T(8,128)(2,1)S(1)}, u32[]{:S(2)}, u32[]{:S(2)}) %all-to-all-start.5) | async-done | bytes 1310752 | tf_op jit(solution)/shard_map/all_to_all | solution.py:137
  (55 shorter events, 25.0 us)
Async XLA Ops:
  0.0 405.5 %copy-start = (bf16[2048,16]{0,1:T(8,128)(2,1)S(1)}, bf16[2048,16]{0,1:T(8,128)(2,1)}, u32[]{:S(2)}) copy-start(bf16[2048,16]{0,1:T(8,128)(2,1)} %param.17) | copy-start | bytes 196612
  1.9 13.0 %copy-start.11 = (s32[16]{0:T(128)S(1)}, s32[16]{0:T(128)}, u32[]{:S(2)}) copy-start(s32[16]{0:T(128)} %constant.67.clone) | copy-start | bytes 196
  7.5 21.9 %all-to-all-start = ((bf16[16,2,8192]{2,1,0:T(2,128)(2,1)}), bf16[16,2,8192]{2,1,0:T(2,128)(2,1)S(1)}, u32[]{:S(2)}, u32[]{:S(2)}) async-start(bf16[16,2,8192]{2,1,0:T(2,128)(2,1)} %reshape.305), calls=%async_computation | async-start | bytes 1048576 | tf_op jit(solution)/shard_map/all_to_all | solution.py:72
  30.4 0.7 copy-start.6
  31.1 2.0 copy-start.8
  45.1 82.1 %all-to-all-start.1 = ((f32[2,2,16,8,2048]{4,3,1,0,2:T(8,128)}), f32[2,2,16,8,2048]{4,3,1,0,2:T(8,128)}, u32[]{:S(2)}, u32[]{:S(2)}) async-start(f32[2,2,16,8,2048]{4,3,1,0,2:T(8,128)} %copy.64), calls=%async_computation.1 | async-start | bytes 8388608 | tf_op jit(solution)/shard_map/all_to_all | solution.py:86
  54.9 74.8 %copy-start.2 = (f32[128,128,1]{1,0,2:T(8,128)S(1)}, f32[128,128,1]{1,0,2:T(8,128)}, u32[]{:S(2)}) copy-start(f32[128,128,1]{1,0,2:T(8,128)} %constant.74) | copy-start | bytes 196612
  133.2 3.5 copy-start.5
  136.7 3.5 copy-start.1
  146.0 1.9 copy-start.4
  282.4 5.1 %copy-start.7 = (f32[16,16,1,1]{0,1,3,2:T(8,128)S(1)}, f32[16,16,1,1]{0,1,3,2:T(8,128)}, u32[]{:S(2)}) copy-start(f32[16,16,1,1]{0,1,3,2:T(8,128)} %constant.77) | copy-start | bytes 3076
  297.4 6.9 %copy-start.9 = (s32[2,128]{1,0:T(2,128)S(1)}, s32[2,128]{1,0:T(2,128)}, u32[]{:S(2)}) copy-start(s32[2,128]{1,0:T(2,128)} %param.21) | copy-start | bytes 3076
  297.4 6.9 %copy-start.10 = (s32[2,128]{1,0:T(2,128)S(1)}, s32[2,128]{1,0:T(2,128)}, u32[]{:S(2)}) copy-start(s32[2,128]{1,0:T(2,128)} %param.22) | copy-start | bytes 3076
  297.4 29.8 %copy-start.3 = (bf16[128,2048]{1,0:T(8,128)(2,1)S(1)}, bf16[128,2048]{1,0:T(8,128)(2,1)}, u32[]{:S(2)}) copy-start(bf16[128,2048]{1,0:T(8,128)(2,1)} %param.15) | copy-start | bytes 1572868
  299.0 28.2 %all-to-all-start.3 = ((f32[16,8,2048]{2,1,0:T(8,128)}), f32[16,8,2048]{2,1,0:T(8,128)S(1)}, u32[]{:S(2)}, u32[]{:S(2)}) async-start(f32[16,8,2048]{2,1,0:T(8,128)} %copy.81), calls=%async_computation.3 | async-start | bytes 2097152 | tf_op jit(solution)/shard_map/all_to_all | solution.py:98
  400.4 37.0 %all-to-all-start.5 = ((bf16[16,20,2048]{2,1,0:T(8,128)(2,1)}), bf16[16,20,2048]{2,1,0:T(8,128)(2,1)S(1)}, u32[]{:S(2)}, u32[]{:S(2)}) async-start(bf16[16,20,2048]{2,1,0:T(8,128)(2,1)} %reshape.294), calls=%async_computation.5 | async-start | bytes 3145728 | tf_op jit(solution)/shard_map/all_to_all | solution.py:137
where the time goes:
time: 448 us; the launch traced here: 440 us
  blocking collectives  155 us (35%)
  waiting for transfers between devices  141 us (31%)
  matrix products  77.9 us (17%)
  local copies, waits for them, and re-layouts  32.6 us (7%)
  starting transfers between devices  22.2 us (5%)
  other arithmetic  10.5 us (2%)
    all_to_all x1, blocking collectives, local(): lax.all_to_all(signal.reshape(2, 2, 1, tok_rows, channels), 'ctx', split_...  112 us
    all_to_all x1, waiting for transfers between devices, local(): lax.all_to_all(spread, 'ctx', split_axis=2, concat_axis=3, tiled=True)  72.3 us
    all_to_all x1, blocking collectives, local(): lax.all_to_all(outgoing, 'ctx', split_axis=0, concat_axis=0, tiled=True)  42.9 us
    all_to_all x1, waiting for transfers between devices, local(): lax.all_to_all(partial_value.reshape(slot_rows.shape), 'ctx', split_axis=...  31.6 us
    all_to_all x1, waiting for transfers between devices, local(): lax.all_to_all(folded, 'ctx', split_axis=0, concat_axis=1, tiled=True)  22.9 us
    dot_general x1, matrix products, local(): jnp.dot(hidden, w_down, preferred_element_type=jnp.float32)  16.3 us
    all_to_all x1, waiting for transfers between devices, local(): lax.all_to_all(value_stream.reshape(1, tok_rows, channels), 'ctx', split_...  14.3 us
    dot_general x4, matrix products, mix_form(): jnp.einsum(form, table_re, stacked[0], precision=highest)  12.9 us
  transfers between devices with their start and end apart: 4, of which 4 were waited for; matrix products, arithmetic and copies ran while one was open for 1% of the time, Pallas kernels for 0%

commit v1 on v0

v1 whole, which is shorter than its diff:
```python
import jax
import jax.numpy as jnp
import numpy as np
from jax import lax
from jax.sharding import PartitionSpec as P

CAP = 20


two_pi = 2.0 * np.pi
highest = lax.Precision.HIGHEST


def reverse_bits(length_n):
    bit_count = length_n.bit_length() - 1
    positions = np.arange(length_n)
    reversed_index = np.zeros(length_n, dtype=np.int64)
    for position in range(bit_count):
        reversed_index = reversed_index | (positions >> position & 1) << bit_count - 1 - position
    return reversed_index


def spread_table(size_ctx):
    rho = 2 * reverse_bits(size_ctx)[None, :] + np.arange(2)[:, None]
    angle_rad = -two_pi * (np.outer(rho.reshape(-1), np.arange(size_ctx)) % (2 * size_ctx)) / (2 * size_ctx)
    parts = np.stack([np.cos(angle_rad), np.sin(angle_rad)], axis=1)
    return jnp.asarray(parts, jnp.float32)


def fine_table(size_ctx, tok_rows):
    total = 2 * size_ctx * tok_rows
    rho = (2 * reverse_bits(size_ctx)[None, :] + np.arange(2)[:, None]).reshape(-1)
    k = 2 * size_ctx * reverse_bits(tok_rows)[None, :] + rho[:, None]
    step = (k[:, :, None] * np.arange(tok_rows)[None, None, :]) % total
    angle_rad = -two_pi * step / total
    re, im = np.cos(angle_rad), np.sin(angle_rad)
    table = np.stack([np.stack([re, -im], axis=2), np.stack([im, re], axis=2)], axis=1)
    return jnp.asarray(table.reshape(2 * size_ctx, 2 * tok_rows, 2 * tok_rows), jnp.float32)


def convolve(arrived, filter_all, size_ctx, tok_rows, block):
    rho_count = 2 * size_ctx
    coarse = spread_table(size_ctx)
    fine = fine_table(size_ctx, tok_rows)
    samples = arrived.astype(jnp.float32).reshape(size_ctx, tok_rows * block)
    spread = jnp.dot(coarse.reshape(2 * rho_count, size_ctx), samples, precision=highest)
    spread = spread.reshape(rho_count, 2 * tok_rows, block)
    signal = jnp.einsum("rqt,rtc->rqc", fine, spread, precision=highest)
    signal = signal.reshape(rho_count, 2, tok_rows, block)
    filter32 = filter_all.astype(jnp.float32).reshape(2, rho_count, tok_rows, block)
    real_part = signal[:, 0] * filter32[0] - signal[:, 1] * filter32[1]
    imag_part = signal[:, 0] * filter32[1] + signal[:, 1] * filter32[0]
    signal = jnp.concatenate([real_part, imag_part], axis=1)
    spread = jnp.einsum("rqt,rqc->rtc", fine, signal, precision=highest)
    spread = spread.reshape(2 * rho_count, tok_rows * block)
    folded = jnp.dot(coarse.reshape(2 * rho_count, size_ctx).T, spread, precision=highest)
    return (folded / (rho_count * tok_rows)).reshape(size_ctx * tok_rows, block)


def local(
    value_stream, gate_stream, filter_spectrum, router, w_gate, w_up, w_down, route_ids, route_slots
):
    tok_rows, channels = value_stream.shape
    size_ctx = lax.axis_size("ctx")
    block = channels // size_ctx
    arrived = lax.all_to_all(value_stream, "ctx", split_axis=1, concat_axis=0, tiled=True)
    filter_all = lax.all_to_all(filter_spectrum, "ctx", split_axis=3, concat_axis=2, tiled=True)
    long_conv = convolve(arrived, filter_all, size_ctx, tok_rows, block)
    long_conv = lax.all_to_all(
        long_conv.astype(jnp.bfloat16), "ctx", split_axis=0, concat_axis=1, tiled=True
    ).astype(jnp.float32)
    hyena_out = (gate_stream.astype(jnp.float32) * long_conv).astype(jnp.bfloat16)
    hyena32 = hyena_out.astype(jnp.float32)
    inv_rms = lax.rsqrt(jnp.mean(hyena32 * hyena32, axis=1, keepdims=True) + 1e-06)
    normed = (hyena32 * inv_rms).astype(jnp.bfloat16)
    logits = jnp.dot(normed, router, preferred_element_type=jnp.float32)
    expert_count = router.shape[1]
    owner_split = size_ctx // expert_count
    slot_count = expert_count * CAP
    positions = jnp.arange(slot_count, dtype=jnp.int32)
    expert_range = jnp.arange(expert_count, dtype=jnp.int32)
    combine = jnp.zeros((tok_rows, slot_count), jnp.float32)
    dispatch = jnp.zeros((slot_count, channels), jnp.float32)
    for pick_index in range(route_ids.shape[0]):
        expert_ids = route_ids[pick_index]
        slot_ids = route_slots[pick_index]
        target = jnp.where(slot_ids < CAP, expert_ids * CAP + slot_ids, -1)
        slot_hits = target[:, None] == positions[None, :]
        chosen_logit = jnp.sum(
            jnp.where(expert_ids[:, None] == expert_range[None, :], logits, 0.0), axis=1
        )
        gate_value = jax.nn.sigmoid(chosen_logit)
        combine = combine + slot_hits.astype(jnp.float32) * gate_value[:, None]
        dispatch = dispatch + lax.dot_general(
            slot_hits.astype(jnp.bfloat16),
            normed,
            (((0,), (0,)), ((), ())),
            preferred_element_type=jnp.float32,
        )
    buffer = dispatch.astype(jnp.bfloat16).reshape(expert_count, CAP, channels)
    outgoing = jnp.repeat(buffer, owner_split, axis=0)
    slot_rows = lax.all_to_all(outgoing, "ctx", split_axis=0, concat_axis=0, tiled=True)
    flat_rows = slot_rows.reshape(-1, channels)
    gate_part = jnp.dot(flat_rows, w_gate, preferred_element_type=jnp.float32)
    up_part = jnp.dot(flat_rows, w_up, preferred_element_type=jnp.float32)
    hidden = (jax.nn.silu(gate_part) * up_part).astype(jnp.bfloat16)
    partial_value = jnp.dot(hidden, w_down, preferred_element_type=jnp.float32).astype(jnp.bfloat16)
    returned = lax.all_to_all(
        partial_value.reshape(slot_rows.shape), "ctx", split_axis=0, concat_axis=0, tiled=True
    )
    expert_out = jnp.sum(
        returned.astype(jnp.float32).reshape(expert_count, owner_split, CAP, channels), axis=1
    ).reshape(slot_count, channels)
    contribution = jnp.dot(combine, expert_out, precision=highest)
    return (hyena32 + contribution).astype(jnp.bfloat16)


def solution(mesh):
    in_specs = (
        P(("groups", "ctx"), None),
        P(("groups", "ctx"), None),
        P(None, None, "ctx", None),
        P(),
        P(None, "ctx"),
        P(None, "ctx"),
        P("ctx", None),
        P(None, ("groups", "ctx")),
        P(None, ("groups", "ctx")),
    )
    out_specs = P(("groups", "ctx"), None)
    return jax.shard_map(local, mesh=mesh, in_specs=in_specs, out_specs=out_specs, check_vma=False)
```

time: 448 us -> 254 us (0.57)
  blocking collectives: 155 us -> 40.1 us
  waiting for transfers between devices: 141 us -> 73.3 us
  matrix products: 77.9 us -> 68.6 us
  other arithmetic: 10.5 us -> 1.36 us
  starting transfers between devices: 22.2 us -> 27.7 us
  local copies, waits for them, and re-layouts: 32.6 us -> 38 us
    all_to_all x1 -> x0, blocking collectives: 112 us -> none  [local(): lax.all_to_all(signal.reshape(2, 2, 1, tok_rows, channels), 'ctx', split_...]
    all_to_all x3, waiting for transfers between devices: 110 us -> 41.7 us  [the longest x1 19 us: local(): lax.all_to_all(filter_spectrum, 'ctx', split_axis=3, concat_axis=2, tiled...]
    dot_general x16 -> x4, matrix products: 49.6 us -> 36.9 us  [the longest x1 15.2 us: convolve(): spread = jnp.einsum('rqt,rqc->rtc', fine, signal, precision=highest)]
    all_to_all x3, starting transfers between devices: 17.2 us -> 22.7 us  [the longest x1 11.2 us: local(): lax.all_to_all(long_conv.astype(jnp.bfloat16), 'ctx', split_axis=0, conca...]
    convert_element_type x0 -> x1, local copies, waits for them, and re-layouts: none -> 5.02 us  [convolve(): filter_all.astype(jnp.float32).reshape(2, rho_count, tok_rows, block)]
    unnamed x28 -> x22, local copies, waits for them, and re-layouts: 5.68 us -> 10.6 us
    another operation x1 -> x0, local copies, waits for them, and re-layouts: 4.63 us -> none  [complex_times(): return jnp.stack([real_part, imag_part])]
  transfers between devices with their start and end apart: 4 -> 4, of which waited for: 4 -> 4; matrix products, arithmetic and copies ran while one was open for 1% -> 11% of each run, Pallas kernels for 0% -> 0%
where the time goes in v1:
time: 254 us; the launch traced here: 249 us
  waiting for transfers between devices  73.3 us (29%)
  matrix products  68.6 us (27%)
  blocking collectives  40.1 us (16%)
  local copies, waits for them, and re-layouts  38 us (15%)
  starting transfers between devices  27.7 us (11%)
    all_to_all x1, blocking collectives, local(): lax.all_to_all(outgoing, 'ctx', split_axis=0, concat_axis=0, tiled=True)  40.1 us
    all_to_all x1, waiting for transfers between devices, local(): lax.all_to_all(partial_value.reshape(slot_rows.shape), 'ctx', split_axis=...  31.6 us
    all_to_all x1, waiting for transfers between devices, local(): lax.all_to_all(filter_spectrum, 'ctx', split_axis=3, concat_axis=2, tiled...  19 us
    dot_general x1, matrix products, local(): jnp.dot(hidden, w_down, preferred_element_type=jnp.float32)  17.4 us
    dot_general x1, matrix products, convolve(): spread = jnp.einsum('rqt,rqc->rtc', fine, signal, precision=highest)  15.2 us
    all_to_all x1, waiting for transfers between devices, local(): lax.all_to_all(long_conv.astype(jnp.bfloat16), 'ctx', split_axis=0, conca...  14.4 us
    dot_general x1, matrix products, convolve(): signal = jnp.einsum('rqt,rtc->rqc', fine, spread, precision=highest)  13.5 us
    all_to_all x1, starting transfers between devices, local(): lax.all_to_all(long_conv.astype(jnp.bfloat16), 'ctx', split_axis=0, conca...  11.2 us
  transfers between devices with their start and end apart: 4, of which 4 were waited for; matrix products, arithmetic and copies ran while one was open for 11% of the time, Pallas kernels for 0%

profile of v1, /device:TPU:0, one launch (start us, length us, event | category | flops | bytes accessed | tf_op | source)
XLA Modules:
  0.0 249.3 jit_solution(3457159549754882394)
XLA Ops:
  0.0 1.0 copy-done
  1.0 0.9 copy_bitcast_fusion
  2.0 7.4 %all-to-all-start = ((bf16[128,16,128]{2,0,1:T(8,128)(2,1)}), bf16[128,16,128]{2,0,1:T(8,128)(2,1)S(1)}, u32[]{:S(2)}, u32[]{:S(2)}) async-start(bf16[128,16,128]{2,0,1:T(8,128)(2,1)} %copy_bitcast_fusion), calls=%async_computation | async-start | bytes 1048576 | tf_op jit(solution)/shard_map/all_to_all | solution.py:66
  9.4 6.2 %copy.25 = bf16[2,2,128,2048]{2,1,0,3:T(2,128)(2,1)} copy(bf16[2,2,128,2048]{3,2,1,0:T(8,128)(2,1)} %param.13) | data formatting | bytes 4194304 | tf_op args[2]
  15.6 8.3 %all-to-all-done = bf16[128,16,128]{2,0,1:T(8,128)(2,1)S(1)} async-done(((bf16[128,16,128]{2,0,1:T(8,128)(2,1)}), bf16[128,16,128]{2,0,1:T(8,128)(2,1)S(1)}, u32[]{:S(2)}, u32[]{:S(2)}) %all-to-all-start) | async-done | bytes 524320 | tf_op jit(solution)/shard_map/all_to_all | solution.py:66
  23.8 4.1 %all-to-all-start.1 = ((bf16[2,2,128,2048]{2,1,0,3:T(2,128)(2,1)}), bf16[2,2,128,2048]{2,1,0,3:T(2,128)(2,1)S(1)}, u32[]{:S(2)}, u32[]{:S(2)}) async-start(bf16[2,2,128,2048]{2,1,0,3:T(2,128)(2,1)} %copy.25), calls=%async_computation.1 | async-start | bytes 4194304 | tf_op jit(solution)/shard_map/all_to_all | solution.py:67
  27.9 3.7 %fusion.14 = f32[64,16384]{1,0:T(8,128)} fusion(f32[64,16]{1,0:T(8,128)S(1)} %copy-done.4, bf16[2,8,128,128]{3,2,1,0:T(8,128)(2,1)S(1)} %bitcast.93), kind=kOutput, calls=%fused_computation.29 | convolution fusion | flops 201326592 | bytes 4722688 | tf_op jit(solution)/shard_map/dot_general | solution.py:46
  31.7 4.9 %reshape.107 = f32[32,256,128]{2,1,0:T(8,128)} reshape(f32[64,16384]{1,0:T(8,128)} %fusion.14) | data formatting | bytes 8388608 | tf_op jit(solution)/shard_map/reshape | solution.py:47
  36.6 13.5 %fusion.37 = f32[32,256,128]{2,1,0:T(8,128)} fusion(f32[32,256,256]{2,1,0:T(8,128)} %constant.25.clone, f32[32,256,128]{2,1,0:T(8,128)} %reshape.107), kind=kOutput, calls=%fused_computation.64 | convolution fusion | flops 3221225472 | bytes 16777216 | tf_op jit(solution)/shard_map/rqt,rtc->rqc/dot_general | solution.py:48
  50.1 19.0 %all-to-all-done.1 = bf16[2,2,128,2048]{2,1,0,3:T(2,128)(2,1)S(1)} async-done(((bf16[2,2,128,2048]{2,1,0,3:T(2,128)(2,1)}), bf16[2,2,128,2048]{2,1,0,3:T(2,128)(2,1)S(1)}, u32[]{:S(2)}, u32[]{:S(2)}) %all-to-all-start.1) | async-done | bytes 2097184 | tf_op jit(solution)/shard_map/all_to_all | solution.py:67
  69.0 5.0 %copy.26 = f32[2,2,128,16,128]{4,2,3,1,0:T(8,128)} copy(bf16[2,2,128,16,128]{2,1,0,4,3:T(2,128)(2,1)S(1)} %bitcast.92) | data formatting | bytes 6291456 | tf_op jit(solution)/shard_map/convert_element_type | solution.py:50
  74.1 2.6 %fusion.36 = (f32[1,2,16,128,128]{4,3,2,1,0:T(8,128)S(1)}, f32[1,2,16,128,128]{4,3,2,1,0:T(8,128)S(1)}) fusion(f32[2,2,16,128,128]{4,3,2,1,0:T(8,128)} %bitcast.91), kind=kLoop, calls=%fused_computation.63 | loop fusion | bytes 8388608 | tf_op jit(solution)/shard_map/slice | solution.py:51
  76.7 0.8 copy-done.2
  77.5 1.1 fusion.8
  78.8 1.4 slice-done.1
  80.2 15.2 %fusion.1 = f32[32,256,128]{2,1,0:T(8,128)} fusion(f32[32,256,256]{2,1,0:T(8,128)S(1)} %bitcast.89, f32[32,128,128]{2,1,0:T(8,128)S(1)} %get-tuple-element.10, f32[32,128,128]{2,1,0:T(8,128)S(1)} %get-tuple-element.9), kind=kOutput, calls=%fused_computation.3 | convolution fusion | flops 3222274048 | bytes 16777216 | tf_op jit(solution)/shard_map/rqt,rqc->rtc/dot_general | solution.py:54
  95.4 5.0 %reshape.109 = f32[64,16384]{1,0:T(8,128)} reshape(f32[32,256,128]{2,1,0:T(8,128)} %fusion.1) | data formatting | bytes 8388608 | tf_op jit(solution)/shard_map/reshape | solution.py:55
  100.4 4.5 %fusion.10 = bf16[2,8,128,128]{3,1,2,0:T(8,128)(2,1)S(1)} fusion(f32[64,16384]{1,0:T(8,128)} %reshape.109, f32[64,16]{1,0:T(8,128)S(1)} %copy-done.4), kind=kOutput, calls=%fused_computation.23 | convolution fusion | flops 201850880 | bytes 4722688 | tf_op jit(solution)/shard_map/dot_general | solution.py:56
  104.9 0.9 copy.36
  105.8 11.2 %all-to-all-start.2 = ((bf16[16,128,128]{2,1,0:T(8,128)(2,1)}), bf16[16,128,128]{2,1,0:T(8,128)(2,1)S(1)}, u32[]{:S(2)}, u32[]{:S(2)}) async-start(bf16[16,128,128]{2,1,0:T(8,128)(2,1)} %bitcast.26), calls=%async_computation.2 | async-start | bytes 1048576 | tf_op jit(solution)/shard_map/all_to_all | solution.py:69
  117.0 14.4 %all-to-all-done.2 = bf16[16,128,128]{2,1,0:T(8,128)(2,1)S(1)} async-done(((bf16[16,128,128]{2,1,0:T(8,128)(2,1)}), bf16[16,128,128]{2,1,0:T(8,128)(2,1)S(1)}, u32[]{:S(2)}, u32[]{:S(2)}) %all-to-all-start.2) | async-done | bytes 524320 | tf_op jit(solution)/shard_map/all_to_all | solution.py:69
  132.4 1.7 fusion.6
  134.2 2.2 reshape_broadcast_in_dim_reshape.3
  136.4 40.1 %all_to_all.45 = bf16[16,20,2048]{2,1,0:T(8,128)(2,1)} all-to-all(bf16[16,20,2048]{2,1,0:T(8,128)(2,1)S(1)} %reshape_broadcast_in_dim_reshape.3), channel_id=1, replica_groups=mesh['groups'=2,'ctx'=16] {'ctx'}, dimensions={0} | all-to-all | bytes 2621440 | tf_op jit(solution)/shard_map/all_to_all | solution.py:102
  176.5 2.3 reshape.110
  178.7 8.5 %fusion.38 = f32[320,2816]{1,0:T(8,128)} fusion(bf16[320,2048]{1,0:T(8,128)(2,1)S(1)} %reshape.110, bf16[2048,2816]{1,0:T(8,128)(2,1)} %param.15), kind=kOutput, calls=%fused_computation.65 | convolution fusion | flops 3690987520 | bytes 16449536 | tf_op jit(solution)/shard_map/dot_general | solution.py:104
  187.2 17.4 %convolution_convert_fusion = bf16[320,2048]{1,0:T(8,128)(2,1)} fusion(bf16[2816,2048]{1,0:T(8,128)(2,1)} %param.17, bf16[320,2048]{1,0:T(8,128)(2,1)S(1)} %reshape.110, bf16[2048,2816]{1,0:T(8,128)(2,1)} %param.16, f32[320,2816]{1,0:T(8,128)} %fusion.38), kind=kOutput, calls=%fused_computation.10 | convolution fusion | flops 7388037120 | bytes 29294592 | tf_op jit(solution)/shard_map/dot_general | solution.py:107
  204.6 3.2 %reshape.111 = bf16[16,20,2048]{2,1,0:T(8,128)(2,1)} reshape(bf16[320,2048]{1,0:T(8,128)(2,1)} %convolution_convert_fusion) | data formatting | bytes 2621440 | tf_op jit(solution)/shard_map/reshape | solution.py:109
  207.9 5.0 %all-to-all-start.4 = ((bf16[16,20,2048]{2,1,0:T(8,128)(2,1)}), bf16[16,20,2048]{2,1,0:T(8,128)(2,1)S(1)}, u32[]{:S(2)}, u32[]{:S(2)}) async-start(bf16[16,20,2048]{2,1,0:T(8,128)(2,1)} %reshape.111), calls=%async_computation.4 | async-start | bytes 3145728 | tf_op jit(solution)/shard_map/all_to_all | solution.py:108
  213.3 31.6 %all-to-all-done.4 = bf16[16,20,2048]{2,1,0:T(8,128)(2,1)S(1)} async-done(((bf16[16,20,2048]{2,1,0:T(8,128)(2,1)}), bf16[16,20,2048]{2,1,0:T(8,128)(2,1)S(1)}, u32[]{:S(2)}, u32[]{:S(2)}) %all-to-all-start.4) | async-done | bytes 1310752 | tf_op jit(solution)/shard_map/all_to_all | solution.py:108
  244.9 1.2 reshape.112
  246.1 3.2 %fusion.7 = bf16[128,2048]{1,0:T(8,128)(2,1)} fusion(bf16[320,2048]{1,0:T(8,128)(2,1)} %reshape.112, bf16[128,2048]{1,0:T(8,128)(2,1)S(1)} %get-tuple-element.8, f32[128]{0:T(128)S(1)} %get-tuple-element.17, s32[128]{0:T(128)S(1)} %get-tuple-element.13, f32[128]{0:T(128)S(1)} %get-tuple-element.18, s32[128]{0:T(128)S(1)} %get-tuple-element.14), kind=kOutput, calls=%fused_computation.12 | convolution fusion | flops 1007624192 | bytes 2361344 | tf_op jit(solution)/shard_map/dot_general | solution.py:114
  (25 shorter events, 1.5 us)
Async XLA Ops:
  0.0 1.0 copy-start
  2.0 21.9 %all-to-all-start = ((bf16[128,16,128]{2,0,1:T(8,128)(2,1)}), bf16[128,16,128]{2,0,1:T(8,128)(2,1)S(1)}, u32[]{:S(2)}, u32[]{:S(2)}) async-start(bf16[128,16,128]{2,0,1:T(8,128)(2,1)} %copy_bitcast_fusion), calls=%async_computation | async-start | bytes 1048576 | tf_op jit(solution)/shard_map/all_to_all | solution.py:66
  9.4 18.6 %copy-start.4 = (f32[64,16]{1,0:T(8,128)S(1)}, f32[64,16]{1,0:T(8,128)}, u32[]{:S(2)}) copy-start(f32[64,16]{1,0:T(8,128)} %constant.26) | copy-start | bytes 12292
  23.8 45.2 %all-to-all-start.1 = ((bf16[2,2,128,2048]{2,1,0,3:T(2,128)(2,1)}), bf16[2,2,128,2048]{2,1,0,3:T(2,128)(2,1)S(1)}, u32[]{:S(2)}, u32[]{:S(2)}) async-start(bf16[2,2,128,2048]{2,1,0,3:T(2,128)(2,1)} %copy.25), calls=%async_computation.1 | async-start | bytes 4194304 | tf_op jit(solution)/shard_map/all_to_all | solution.py:67
  74.1 3.4 %copy-start.2 = (f32[32,256,128]{2,1,0:T(8,128)S(1)}, f32[32,256,128]{2,1,0:T(8,128)}, u32[]{:S(2)}) copy-start(f32[32,256,128]{2,1,0:T(8,128)} %fusion.37) | copy-start | bytes 12582916
  74.1 4.7 %slice-start = ((s8[8388608]{0:T(1024)(128)(4,1)}), s8[4194304]{0:T(1024)(128)(4,1)S(1)}, s32[]{:S(2)}) async-start(s8[8388608]{0:T(1024)(128)(4,1)} %bitcast.88), calls=%async_computation.5 | async-start | bytes 8388608
  77.5 2.7 %slice-start.1 = ((s8[8388608]{0:T(1024)(128)(4,1)}), s8[4194304]{0:T(1024)(128)(4,1)S(1)}, s32[]{:S(2)}) async-start(s8[8388608]{0:T(1024)(128)(4,1)} %bitcast.88), calls=%async_computation.6 | async-start | bytes 8388608
  100.4 16.6 %copy-start.5 = (s32[2,128]{1,0:T(2,128)S(1)}, s32[2,128]{1,0:T(2,128)}, u32[]{:S(2)}) copy-start(s32[2,128]{1,0:T(2,128)} %param.18) | copy-start | bytes 3076
  100.4 16.6 %copy-start.6 = (s32[2,128]{1,0:T(2,128)S(1)}, s32[2,128]{1,0:T(2,128)}, u32[]{:S(2)}) copy-start(s32[2,128]{1,0:T(2,128)} %param.19) | copy-start | bytes 3076
  100.4 31.1 %copy-start.3 = (bf16[128,2048]{1,0:T(8,128)(2,1)S(1)}, bf16[128,2048]{1,0:T(8,128)(2,1)}, u32[]{:S(2)}) copy-start(bf16[128,2048]{1,0:T(8,128)(2,1)} %param.12) | copy-start | bytes 1572868
  105.8 25.7 %all-to-all-start.2 = ((bf16[16,128,128]{2,1,0:T(8,128)(2,1)}), bf16[16,128,128]{2,1,0:T(8,128)(2,1)S(1)}, u32[]{:S(2)}, u32[]{:S(2)}) async-start(bf16[16,128,128]{2,1,0:T(8,128)(2,1)} %bitcast.26), calls=%async_computation.2 | async-start | bytes 1048576 | tf_op jit(solution)/shard_map/all_to_all | solution.py:69
  204.6 8.3 %copy-start.7 = (bf16[2048,16]{0,1:T(8,128)(2,1)S(1)}, bf16[2048,16]{0,1:T(8,128)(2,1)}, u32[]{:S(2)}) copy-start(bf16[2048,16]{0,1:T(8,128)(2,1)} %param.14) | copy-start | bytes 196612
  207.9 37.0 %all-to-all-start.4 = ((bf16[16,20,2048]{2,1,0:T(8,128)(2,1)}), bf16[16,20,2048]{2,1,0:T(8,128)(2,1)S(1)}, u32[]{:S(2)}, u32[]{:S(2)}) async-start(bf16[16,20,2048]{2,1,0:T(8,128)(2,1)} %reshape.111), calls=%async_computation.4 | async-start | bytes 3145728 | tf_op jit(solution)/shard_map/all_to_all | solution.py:108
  212.9 36.4 %copy-start.1 = (bf16[128,2048]{1,0:T(8,128)(2,1)S(1)}, bf16[128,2048]{1,0:T(8,128)(2,1)}, u32[]{:S(2)}) copy-start(bf16[128,2048]{1,0:T(8,128)(2,1)} %param.11) | copy-start | bytes 1572868

commit v2 on v1

--- a/solution.py
+++ b/solution.py
@@ -2,6 +2,8 @@
 import jax.numpy as jnp
 import numpy as np
 from jax import lax
+from jax.experimental import pallas as pl
+from jax.experimental.pallas import tpu as pltpu
 from jax.sharding import PartitionSpec as P
 
 CAP = 20
@@ -57,6 +59,229 @@
     return (folded / (rho_count * tok_rows)).reshape(size_ctx * tok_rows, block)
 
 
+def flip_bits(index, mask):
+    result = index
+    bit = 1
+    while bit <= mask:
+        if mask & bit:
+            result = result + bit * (1 - 2 * ((index // bit) % 2))
+        bit *= 2
+    return result
+
+
+MASKS = (0, 1, 2, 3, 8, 9, 10, 11, 4, 5, 6, 7, 12, 13, 14, 15)
+HEAD = 16
+TAIL = CAP - HEAD
+QUARTERS = HEAD // TAIL
+
+
+def expert_kernel(
+    conv_ref, stream_ref, router_ref, ids_ref, head_ref, tail_ref, wg_hbm, wu_hbm, wd_hbm, out_ref,
+    hyena, send_head, send_tail, recv_head, recv_tail, done_head, done_tail, back_head, back_tail,
+    rows, hidden, wg, wu, wd, tail_sum, gates, own_sem, send_sem, recv_sem, weight_sem,
+):
+    device = lax.axis_index("ctx")
+    peers = [flip_bits(device, mask) for mask in MASKS]
+    count = len(MASKS)
+    channels = conv_ref.shape[1]
+    quarter = channels // QUARTERS
+    tokens = conv_ref.shape[0]
+    slots = count * HEAD
+    weights = [
+        pltpu.make_async_copy(src, dst, weight_sem.at[i])
+        for i, (src, dst) in enumerate(((wg_hbm, wg), (wu_hbm, wu), (wd_hbm, wd)))
+    ]
+    for copy in weights:
+        copy.start()
+    barrier = pltpu.get_barrier_semaphore()
+    for slot in range(1, count):
+        pl.semaphore_signal(
+            barrier, inc=1, device_id={"ctx": peers[slot]}, device_id_type=pl.DeviceIdType.MESH
+        )
+    mixed = (stream_ref[...].astype(jnp.float32) * conv_ref[...].astype(jnp.float32)).astype(jnp.bfloat16)
+    hyena[...] = mixed
+    mixed32 = mixed.astype(jnp.float32)
+    mean = jnp.sum(mixed32 * mixed32, axis=1, keepdims=True) / channels
+    normed = (mixed32 * lax.rsqrt(mean + 1e-06)).astype(jnp.bfloat16)
+    slot_row = lax.broadcasted_iota(jnp.int32, (slots, tokens), 0)
+
+    def hits(targets, shift):
+        return [slot_row == targets[pick : pick + 1, :] + shift for pick in range(2)]
+
+    def one_hot(targets, shift):
+        first, second = hits(targets, shift)
+        return jnp.where(first | second, 1.0, 0.0).astype(jnp.bfloat16)
+
+    head = head_ref[...]
+    tail = tail_ref[...]
+    send_head[...] = jnp.dot(one_hot(head, 0), normed, preferred_element_type=jnp.float32).astype(jnp.bfloat16)
+    packed = jnp.zeros((slots, quarter), jnp.float32)
+    for part in range(QUARTERS):
+        packed = packed + jnp.dot(
+            one_hot(tail, TAIL * part),
+            normed[:, part * quarter : (part + 1) * quarter],
+            preferred_element_type=jnp.float32,
+        )
+    send_tail[...] = packed.astype(jnp.bfloat16)
+    pl.semaphore_wait(barrier, count - 1)
+
+    def exchange(slot, phase):
+        here = pl.ds(slot * HEAD, HEAD)
+        if phase == 0:
+            pairs = ((send_head, recv_head), (send_tail, recv_tail))
+        else:
+            pairs = ((done_head, back_head), (done_tail, back_tail))
+        copies = []
+        for which, (src, dst) in enumerate(pairs):
+            if slot == 0:
+                copies.append(pltpu.make_async_copy(src.at[here], dst.at[here], own_sem.at[phase, which]))
+            else:
+                copies.append(
+                    pltpu.make_async_remote_copy(
+                        src_ref=src.at[here],
+                        dst_ref=dst.at[here],
+                        send_sem=send_sem.at[phase, which, slot],
+                        recv_sem=recv_sem.at[phase, which, slot],
+                        device_id={"ctx": peers[slot]},
+                        device_id_type=pl.DeviceIdType.MESH,
+                    )
+                )
+        return copies
+
+    half = count // 2
+    issue = (7, 6, 5, 4, 3, 2, 1, 0, 15, 14, 13, 12, 11, 10, 9, 8)
+    outward = {slot: exchange(slot, 0) for slot in range(count)}
+    inward = {slot: exchange(slot, 1) for slot in range(count)}
+    for slot in issue:
+        for copy in outward[slot]:
+            copy.start()
+    logits = lax.dot_general(
+        router_ref[...], normed, (((1,), (1,)), ((), ())), preferred_element_type=jnp.float32
+    )
+    expert_row = lax.broadcasted_iota(jnp.int32, logits.shape, 0)
+    ids = ids_ref[...]
+    for pick in range(2):
+        chosen = jnp.sum(
+            jnp.where(expert_row == ids[pick : pick + 1, :], logits, 0.0), axis=0, keepdims=True
+        )
+        gates[pick : pick + 1, :] = jax.nn.sigmoid(chosen)
+    group_rows = half * HEAD
+    tail_rows = half * TAIL
+    pick_row = lax.broadcasted_iota(jnp.int32, (tail_rows, group_rows), 0)
+    pick_col = lax.broadcasted_iota(jnp.int32, (tail_rows, group_rows), 1)
+    pick_base = (pick_row // TAIL) * HEAD + pick_row % TAIL
+    hidden_size = wg.shape[1]
+    for group in range(2):
+        for slot in range(group * half, (group + 1) * half):
+            for copy in outward[slot]:
+                copy.wait()
+        span = pl.ds(group * group_rows, group_rows)
+        rows[0:group_rows, :] = recv_head[span, :]
+        for part in range(QUARTERS):
+            select = jnp.where(pick_col == pick_base + TAIL * part, 1.0, 0.0).astype(jnp.bfloat16)
+            rows[group_rows : group_rows + tail_rows, part * quarter : (part + 1) * quarter] = jnp.dot(
+                select, recv_tail[span, :], preferred_element_type=jnp.float32
+            ).astype(jnp.bfloat16)
+        if group == 0:
+            weights[0].wait()
+            weights[1].wait()
+
+        @pl.loop(0, hidden_size // 256)
+        def _(step):
+            columns = pl.ds(pl.multiple_of(step * 256, 256), 256)
+            gate_part = jnp.dot(rows[...], wg[:, columns], preferred_element_type=jnp.float32)
+            up_part = jnp.dot(rows[...], wu[:, columns], preferred_element_type=jnp.float32)
+            hidden[:, columns] = (jax.nn.silu(gate_part) * up_part).astype(jnp.bfloat16)
+
+        if group == 0:
+            weights[2].wait()
+        tail_sum[...] = jnp.zeros_like(tail_sum)
+
+        @pl.loop(0, QUARTERS)
+        def _(part):
+            columns = pl.ds(pl.multiple_of(part * quarter, 256), quarter)
+            value = jnp.dot(hidden[...], wd[:, columns], preferred_element_type=jnp.float32).astype(jnp.bfloat16)
+            done_head[span, columns] = value[0:group_rows, :]
+            select = jnp.where(pick_col == pick_base + TAIL * part, 1.0, 0.0).astype(jnp.bfloat16)
+            tail_sum[...] += lax.dot_general(
+                select,
+                value[group_rows : group_rows + tail_rows, :],
+                (((0,), (0,)), ((), ())),
+                preferred_element_type=jnp.float32,
+            )
+
+        done_tail[span, :] = tail_sum[...].astype(jnp.bfloat16)
+        for slot in issue[group * half : (group + 1) * half]:
+            for copy in inward[slot]:
+                copy.start()
+
+    def weighted(targets, shift, values):
+        first, second = hits(targets, shift)
+        mix = jnp.where(first, gates[0:1, :], 0.0) + jnp.where(second, gates[1:2, :], 0.0)
+        high = mix.astype(jnp.bfloat16)
+        low = (mix - high.astype(jnp.float32)).astype(jnp.bfloat16)
+        dims = (((0,), (0,)), ((), ()))
+        return lax.dot_general(high, values, dims, preferred_element_type=jnp.float32) + lax.dot_general(
+            low, values, dims, preferred_element_type=jnp.float32
+        )
+
+    for slot in range(count):
+        for copy in inward[slot]:
+            copy.wait()
+    for part in range(QUARTERS):
+        columns = slice(part * quarter, (part + 1) * quarter)
+        total = hyena[:, columns].astype(jnp.float32)
+        total = total + weighted(head, 0, back_head[:, columns])
+        total = total + weighted(tail, TAIL * part, back_tail[...])
+        out_ref[:, columns] = total.astype(jnp.bfloat16)
+
+
+def run_experts(long_conv, gate_stream, router, w_gate, w_up, w_down, route_ids, route_slots):
+    tokens, channels = gate_stream.shape
+    hidden_size = w_gate.shape[1]
+    count = len(MASKS)
+    slots = count * HEAD
+    half_rows = slots // 2 + (count // 2) * TAIL
+    quarter = channels // QUARTERS
+    device = lax.axis_index("ctx")
+    place = jnp.asarray(np.argsort(np.asarray(MASKS)), jnp.int32)
+    offset = jnp.bitwise_xor(route_ids, device)
+    position = jnp.sum(
+        jnp.where(offset[:, :, None] == jnp.arange(count)[None, None, :], place[None, None, :], 0), axis=2
+    )
+    head = jnp.where(route_slots < HEAD, position * HEAD + route_slots, -1024)
+    tail = jnp.where(
+        (route_slots >= HEAD) & (route_slots < CAP), position * HEAD + route_slots - HEAD, -1024
+    )
+    vmem = pl.BlockSpec(memory_space=pltpu.VMEM)
+    hbm = pl.BlockSpec(memory_space=pl.ANY)
+    bf16 = jnp.bfloat16
+    return pl.pallas_call(
+        expert_kernel,
+        out_shape=jax.ShapeDtypeStruct((tokens, channels), bf16),
+        in_specs=[vmem] * 6 + [hbm] * 3,
+        out_specs=vmem,
+        scratch_shapes=[pltpu.VMEM((tokens, channels), bf16)]
+        + [pltpu.VMEM((slots, channels), bf16), pltpu.VMEM((slots, quarter), bf16)] * 4
+        + [
+            pltpu.VMEM((half_rows, channels), bf16),
+            pltpu.VMEM((half_rows, hidden_size), bf16),
+            pltpu.VMEM((channels, hidden_size), bf16),
+            pltpu.VMEM((channels, hidden_size), bf16),
+            pltpu.VMEM((hidden_size, channels), bf16),
+            pltpu.VMEM((slots // 2, quarter), jnp.float32),
+            pltpu.VMEM((8, tokens), jnp.float32),
+            pltpu.SemaphoreType.DMA((2, 2)),
+            pltpu.SemaphoreType.DMA((2, 2, count)),
+            pltpu.SemaphoreType.DMA((2, 2, count)),
+            pltpu.SemaphoreType.DMA((3,)),
+        ],
+        compiler_params=pltpu.CompilerParams(
+            collective_id=1, has_side_effects=True, vmem_limit_bytes=56 * 1024 * 1024
+        ),
+    )(long_conv, gate_stream, router.T, route_ids, head, tail, w_gate, w_up, w_down)
+
+
 def local(
     value_stream, gate_stream, filter_spectrum, router, w_gate, w_up, w_down, route_ids, route_slots
 ):
@@ -68,13 +293,18 @@
     long_conv = convolve(arrived, filter_all, size_ctx, tok_rows, block)
     long_conv = lax.all_to_all(
         long_conv.astype(jnp.bfloat16), "ctx", split_axis=0, concat_axis=1, tiled=True
-    ).astype(jnp.float32)
+    )
+    expert_count = router.shape[1]
+    if size_ctx == expert_count == len(MASKS) and channels % 512 == 0 and w_gate.shape[1] % 256 == 0:
+        return run_experts(
+            long_conv, gate_stream, router, w_gate, w_up, w_down, route_ids, route_slots
+        )
+    long_conv = long_conv.astype(jnp.float32)
     hyena_out = (gate_stream.astype(jnp.float32) * long_conv).astype(jnp.bfloat16)
     hyena32 = hyena_out.astype(jnp.float32)
     inv_rms = lax.rsqrt(jnp.mean(hyena32 * hyena32, axis=1, keepdims=True) + 1e-06)
     normed = (hyena32 * inv_rms).astype(jnp.bfloat16)
     logits = jnp.dot(normed, router, preferred_element_type=jnp.float32)
-    expert_count = router.shape[1]
     owner_split = size_ctx // expert_count
     slot_count = expert_count * CAP
     positions = jnp.arange(slot_count, dtype=jnp.int32)

time: 254 us -> 202 us (0.80); the launches traced: 249 us -> 201 us
  Pallas kernels: 0 us -> 66.8 us
  blocking collectives: 40.1 us -> 0 us
  waiting for transfers between devices: 73.3 us -> 41 us
  matrix products: 68.6 us -> 36.9 us
  local copies, waits for them, and re-layouts: 38 us -> 31.8 us
  starting transfers between devices: 27.7 us -> 22.7 us
    pallas_call x0 -> x1, Pallas kernels: none -> 66.8 us  [run_experts(): pl.pallas_call(expert_kernel, out_shape=jax.ShapeDtypeStruct((tokens, cha...]
    all_to_all x1 -> x0, blocking collectives: 40.1 us -> none  [local(): lax.all_to_all(outgoing, 'ctx', split_axis=0, concat_axis=0, tiled=True)]
    dot_general x6 -> x0, matrix products: 31.7 us -> none  [the longest x1 17.4 us: local(): jnp.dot(hidden, w_down, preferred_element_type=jnp.float32)]
    all_to_all x1 -> x0, waiting for transfers between devices: 31.6 us -> none  [local(): lax.all_to_all(partial_value.reshape(slot_rows.shape), 'ctx', split_axis=...]
    reshape x3 -> x0, local copies, waits for them, and re-layouts: 6.73 us -> none  [the longest x1 3.22 us: local(): partial_value.reshape(slot_rows.shape)]
    all_to_all x1 -> x0, starting transfers between devices: 5.03 us -> none  [local(): lax.all_to_all(partial_value.reshape(slot_rows.shape), 'ctx', split_axis=...]
    unnamed x22 -> x21, local copies, waits for them, and re-layouts: 10.6 us -> 12.4 us
  transfers between devices with their start and end apart: 4 -> 3, of which waited for: 4 -> 3; matrix products, arithmetic and copies ran while one was open for 11% -> 14% of each run, Pallas kernels for 0% -> 0%
where the time goes in v2:
time: 202 us; the launch traced here: 201 us
  Pallas kernels  66.8 us (33%)
  waiting for transfers between devices  41 us (20%)
  matrix products  36.9 us (18%)
  local copies, waits for them, and re-layouts  31.8 us (16%)
  starting transfers between devices  22.7 us (11%)
    pallas_call x1, Pallas kernels, run_experts(): pl.pallas_call(expert_kernel, out_shape=jax.ShapeDtypeStruct((tokens, cha...  66.8 us
    all_to_all x1, waiting for transfers between devices, local(): lax.all_to_all(filter_spectrum, 'ctx', split_axis=3, concat_axis=2, tiled...  19 us
    dot_general x1, matrix products, convolve(): spread = jnp.einsum('rqt,rqc->rtc', fine, signal, precision=highest)  15.2 us
    all_to_all x1, waiting for transfers between devices, local(): lax.all_to_all(long_conv.astype(jnp.bfloat16), 'ctx', split_axis=0, conca...  13.8 us
    dot_general x1, matrix products, convolve(): signal = jnp.einsum('rqt,rtc->rqc', fine, spread, precision=highest)  13.5 us
    unnamed x21, local copies, waits for them, and re-layouts  12.4 us
    all_to_all x1, starting transfers between devices, local(): lax.all_to_all(long_conv.astype(jnp.bfloat16), 'ctx', split_axis=0, conca...  11.2 us
    all_to_all x1, waiting for transfers between devices, local(): lax.all_to_all(value_stream, 'ctx', split_axis=1, concat_axis=0, tiled=True)  8.29 us
  transfers between devices with their start and end apart: 3, of which 3 were waited for; matrix products, arithmetic and copies ran while one was open for 14% of the time, Pallas kernels for 0%

profile of v2, /device:TPU:0, one launch (start us, length us, event | category | flops | bytes accessed | tf_op | source)
XLA Modules:
  0.0 201.0 jit_solution(1165794785539013409)
XLA Ops:
  0.0 0.0 copy-start
  0.0 1.0 copy-done
  1.0 0.9 copy_bitcast_fusion.1
  2.0 7.4 %all-to-all-start = ((bf16[128,16,128]{2,0,1:T(8,128)(2,1)}), bf16[128,16,128]{2,0,1:T(8,128)(2,1)S(1)}, u32[]{:S(2)}, u32[]{:S(2)}) async-start(bf16[128,16,128]{2,0,1:T(8,128)(2,1)} %copy_bitcast_fusion.1), calls=%async_computation | async-start | bytes 1048576 | tf_op jit(solution)/shard_map/all_to_all | solution.py:291
  9.4 0.0 copy-start.3
  9.4 6.2 %copy.33 = bf16[2,2,128,2048]{2,1,0,3:T(2,128)(2,1)} copy(bf16[2,2,128,2048]{3,2,1,0:T(8,128)(2,1)} %param.14) | data formatting | bytes 4194304 | tf_op args[2]
  15.5 8.3 %all-to-all-done = bf16[128,16,128]{2,0,1:T(8,128)(2,1)S(1)} async-done(((bf16[128,16,128]{2,0,1:T(8,128)(2,1)}), bf16[128,16,128]{2,0,1:T(8,128)(2,1)S(1)}, u32[]{:S(2)}, u32[]{:S(2)}) %all-to-all-start) | async-done | bytes 524320 | tf_op jit(solution)/shard_map/all_to_all | solution.py:291
  23.8 4.1 %all-to-all-start.1 = ((bf16[2,2,128,2048]{2,1,0,3:T(2,128)(2,1)}), bf16[2,2,128,2048]{2,1,0,3:T(2,128)(2,1)S(1)}, u32[]{:S(2)}, u32[]{:S(2)}) async-start(bf16[2,2,128,2048]{2,1,0,3:T(2,128)(2,1)} %copy.33), calls=%async_computation.1 | async-start | bytes 4194304 | tf_op jit(solution)/shard_map/all_to_all | solution.py:292
  27.9 0.0 copy-done.3
  27.9 3.7 %fusion.8 = f32[64,16384]{1,0:T(8,128)} fusion(f32[64,16]{1,0:T(8,128)S(1)} %copy-done.3, bf16[2,8,128,128]{3,2,1,0:T(8,128)(2,1)S(1)} %bitcast.66), kind=kOutput, calls=%fused_computation.15 | convolution fusion | flops 201326592 | bytes 4722688 | tf_op jit(solution)/shard_map/dot_general | solution.py:48
  31.7 4.9 %reshape.42 = f32[32,256,128]{2,1,0:T(8,128)} reshape(f32[64,16384]{1,0:T(8,128)} %fusion.8) | data formatting | bytes 8388608 | tf_op jit(solution)/shard_map/reshape | solution.py:49
  36.6 13.5 %fusion.13 = f32[32,256,128]{2,1,0:T(8,128)} fusion(f32[32,256,256]{2,1,0:T(8,128)} %constant.24.clone, f32[32,256,128]{2,1,0:T(8,128)} %reshape.42), kind=kOutput, calls=%fused_computation.28 | convolution fusion | flops 3221225472 | bytes 16777216 | tf_op jit(solution)/shard_map/rqt,rtc->rqc/dot_general | solution.py:50
  50.1 19.0 %all-to-all-done.1 = bf16[2,2,128,2048]{2,1,0,3:T(2,128)(2,1)S(1)} async-done(((bf16[2,2,128,2048]{2,1,0,3:T(2,128)(2,1)}), bf16[2,2,128,2048]{2,1,0,3:T(2,128)(2,1)S(1)}, u32[]{:S(2)}, u32[]{:S(2)}) %all-to-all-start.1) | async-done | bytes 2097184 | tf_op jit(solution)/shard_map/all_to_all | solution.py:292
  69.0 5.0 %copy.34 = f32[2,2,128,16,128]{4,2,3,1,0:T(8,128)} copy(bf16[2,2,128,16,128]{2,1,0,4,3:T(2,128)(2,1)S(1)} %bitcast.65) | data formatting | bytes 6291456 | tf_op jit(solution)/shard_map/convert_element_type | solution.py:52
  74.1 2.6 %fusion.12 = (f32[1,2,16,128,128]{4,3,2,1,0:T(8,128)S(1)}, f32[1,2,16,128,128]{4,3,2,1,0:T(8,128)S(1)}) fusion(f32[2,2,16,128,128]{4,3,2,1,0:T(8,128)} %bitcast.64), kind=kLoop, calls=%fused_computation.27 | loop fusion | bytes 8388608 | tf_op jit(solution)/shard_map/slice | solution.py:53
  76.7 0.8 copy-done.2
  77.5 1.1 fusion.5
  78.6 0.2 slice-done
  78.8 1.4 slice-done.1
  80.2 15.2 %fusion.1 = f32[32,256,128]{2,1,0:T(8,128)} fusion(f32[32,256,256]{2,1,0:T(8,128)S(1)} %bitcast.62, f32[32,128,128]{2,1,0:T(8,128)S(1)} %get-tuple-element.6, f32[32,128,128]{2,1,0:T(8,128)S(1)} %get-tuple-element.5), kind=kOutput, calls=%fused_computation.2 | convolution fusion | flops 3222274048 | bytes 16777216 | tf_op jit(solution)/shard_map/rqt,rqc->rtc/dot_general | solution.py:56
  95.4 5.0 %reshape.44 = f32[64,16384]{1,0:T(8,128)} reshape(f32[32,256,128]{2,1,0:T(8,128)} %fusion.1) | data formatting | bytes 8388608 | tf_op jit(solution)/shard_map/reshape | solution.py:57
  100.4 4.5 %fusion.7 = bf16[2,8,128,128]{3,1,2,0:T(8,128)(2,1)S(1)} fusion(f32[64,16384]{1,0:T(8,128)} %reshape.44, f32[64,16]{1,0:T(8,128)S(1)} %copy-done.3), kind=kOutput, calls=%fused_computation.14 | convolution fusion | flops 201850880 | bytes 4722688 | tf_op jit(solution)/shard_map/dot_general | solution.py:58
  104.9 0.9 copy.44
  105.8 11.2 %all-to-all-start.2 = ((bf16[16,128,128]{2,1,0:T(8,128)(2,1)}), bf16[16,128,128]{2,1,0:T(8,128)(2,1)S(1)}, u32[]{:S(2)}, u32[]{:S(2)}) async-start(bf16[16,128,128]{2,1,0:T(8,128)(2,1)} %bitcast.23), calls=%async_computation.2 | async-start | bytes 1048576 | tf_op jit(solution)/shard_map/all_to_all | solution.py:294
  117.0 0.0 copy-done.4
  117.0 0.0 copy-done.6
  117.0 0.1 select_reduce_fusion
  117.1 0.6 and_select_fusion
  117.7 13.8 %all-to-all-done.2 = bf16[16,128,128]{2,1,0:T(8,128)(2,1)S(1)} async-done(((bf16[16,128,128]{2,1,0:T(8,128)(2,1)}), bf16[16,128,128]{2,1,0:T(8,128)(2,1)S(1)}, u32[]{:S(2)}, u32[]{:S(2)}) %all-to-all-start.2) | async-done | bytes 524320 | tf_op jit(solution)/shard_map/all_to_all | solution.py:294
  131.5 0.9 copy_bitcast_fusion.conv_ref
  132.3 66.8 %shard_map.118 = bf16[128,2048]{1,0:T(8,128)(2,1)} custom-call(bf16[128,2048]{1,0:T(8,128)(2,1)} %copy_bitcast_fusion.conv_ref, bf16[128,2048]{1,0:T(8,128)(2,1)} %stream_ref.1, bf16[16,2048]{1,0:T(8,128)(2,1)} %bitcast.67, s32[2,128]{1,0:T(2,128)} %ids_ref.1, s32[2,128]{1,0:T(2,128)} %get-tuple-element.10.head_ref, s32[2,128]{1,0:T(2,128)} %get-tuple-element.9.tail_ref, ...), custom_call_target="tpu_custom_call" | custom-call | tf_op jit(solution)/shard_map/pallas_call | solution.py:259
  199.1 1.9 copy.52
  (11 shorter events, 0.0 us)
Async XLA Ops:
  0.0 1.0 copy-start
  2.0 21.9 %all-to-all-start = ((bf16[128,16,128]{2,0,1:T(8,128)(2,1)}), bf16[128,16,128]{2,0,1:T(8,128)(2,1)S(1)}, u32[]{:S(2)}, u32[]{:S(2)}) async-start(bf16[128,16,128]{2,0,1:T(8,128)(2,1)} %copy_bitcast_fusion.1), calls=%async_computation | async-start | bytes 1048576 | tf_op jit(solution)/shard_map/all_to_all | solution.py:291
  9.4 18.6 %copy-start.3 = (f32[64,16]{1,0:T(8,128)S(1)}, f32[64,16]{1,0:T(8,128)}, u32[]{:S(2)}) copy-start(f32[64,16]{1,0:T(8,128)} %constant.26) | copy-start | bytes 12292
  23.8 45.2 %all-to-all-start.1 = ((bf16[2,2,128,2048]{2,1,0,3:T(2,128)(2,1)}), bf16[2,2,128,2048]{2,1,0,3:T(2,128)(2,1)S(1)}, u32[]{:S(2)}, u32[]{:S(2)}) async-start(bf16[2,2,128,2048]{2,1,0,3:T(2,128)(2,1)} %copy.33), calls=%async_computation.1 | async-start | bytes 4194304 | tf_op jit(solution)/shard_map/all_to_all | solution.py:292
  74.1 3.4 %copy-start.2 = (f32[32,256,128]{2,1,0:T(8,128)S(1)}, f32[32,256,128]{2,1,0:T(8,128)}, u32[]{:S(2)}) copy-start(f32[32,256,128]{2,1,0:T(8,128)} %fusion.13) | copy-start | bytes 12582916
  74.1 4.7 %slice-start = ((s8[8388608]{0:T(1024)(128)(4,1)}), s8[4194304]{0:T(1024)(128)(4,1)S(1)}, s32[]{:S(2)}) async-start(s8[8388608]{0:T(1024)(128)(4,1)} %bitcast.61), calls=%async_computation.3 | async-start | bytes 8388608
  77.5 2.7 %slice-start.1 = ((s8[8388608]{0:T(1024)(128)(4,1)}), s8[4194304]{0:T(1024)(128)(4,1)S(1)}, s32[]{:S(2)}) async-start(s8[8388608]{0:T(1024)(128)(4,1)} %bitcast.61), calls=%async_computation.4 | async-start | bytes 8388608
  100.4 16.6 %copy-start.4 = (s32[2,128]{1,0:T(2,128)S(1)}, s32[2,128]{1,0:T(2,128)}, u32[]{:S(2)}) copy-start(s32[2,128]{1,0:T(2,128)} %ids_ref.1) | copy-start | bytes 3076
  100.4 16.6 %copy-start.6 = (s32[16]{0:T(128)S(1)}, s32[16]{0:T(128)}, u32[]{:S(2)}) copy-start(s32[16]{0:T(128)} %constant.25.clone) | copy-start | bytes 196
  100.4 16.7 %copy-start.5 = (s32[2,128]{1,0:T(2,128)S(1)}, s32[2,128]{1,0:T(2,128)}, u32[]{:S(2)}) copy-start(s32[2,128]{1,0:T(2,128)} %param.20) | copy-start | bytes 3076
  105.8 25.7 %all-to-all-start.2 = ((bf16[16,128,128]{2,1,0:T(8,128)(2,1)}), bf16[16,128,128]{2,1,0:T(8,128)(2,1)S(1)}, u32[]{:S(2)}, u32[]{:S(2)}) async-start(bf16[16,128,128]{2,1,0:T(8,128)(2,1)} %bitcast.23), calls=%async_computation.2 | async-start | bytes 1048576 | tf_op jit(solution)/shard_map/all_to_all | solution.py:294
  132.3 68.7 %copy-start.1 = (bf16[128,2048]{1,0:T(8,128)(2,1)S(1)}, bf16[128,2048]{1,0:T(8,128)(2,1)}, u32[]{:S(2)}) copy-start(bf16[128,2048]{1,0:T(8,128)(2,1)} %param.12) | copy-start | bytes 1572868

commit v3 on v2

--- a/solution.py
+++ b/solution.py
@@ -73,6 +73,259 @@
 HEAD = 16
 TAIL = CAP - HEAD
 QUARTERS = HEAD // TAIL
+
+
+def twist_table(size_ctx, tok_rows):
+    rho = (2 * reverse_bits(size_ctx)[:, None] + np.arange(2)[None, :]).reshape(-1)
+    angle_rad = -two_pi * np.outer(np.arange(tok_rows), rho) / (2 * size_ctx * tok_rows)
+    return jnp.asarray(np.concatenate([np.cos(angle_rad), np.sin(angle_rad)], axis=1), jnp.float32)
+
+
+def inner_tables(tok_rows):
+    angle_rad = -two_pi * (np.outer(reverse_bits(tok_rows), np.arange(tok_rows)) % tok_rows) / tok_rows
+    re, im = np.cos(angle_rad), np.sin(angle_rad)
+    table = np.block([[re, -im], [im, re]]).astype(np.float32)
+    pieces = []
+    for matrix in (table, table.T):
+        high = matrix.astype(jnp.bfloat16)
+        low = (matrix - high.astype(np.float32)).astype(jnp.bfloat16)
+        pieces += [high, low]
+    return jnp.asarray(np.stack(pieces))
+
+
+def times_root(pair, power, order):
+    power %= order
+    re, im = pair
+    if power == 0:
+        return pair
+    if im is None and 4 * power % order:
+        cos, sin = float(np.cos(two_pi * power / order)), float(np.sin(two_pi * power / order))
+        return (re * cos, re * sin)
+    if im is None:
+        im = jnp.zeros_like(re)
+    if 4 * power == order:
+        return (-im, re)
+    if 2 * power == order:
+        return (-re, -im)
+    if 4 * power == 3 * order:
+        return (im, -re)
+    cos, sin = float(np.cos(two_pi * power / order)), float(np.sin(two_pi * power / order))
+    return (re * cos - im * sin, re * sin + im * cos)
+
+
+def short_transform(values, sign):
+    order = len(values)
+    if order == 1:
+        return values
+    even = short_transform(values[0::2], sign)
+    odd = short_transform(values[1::2], sign)
+    turned = [times_root(odd[i], sign * i, order) for i in range(order // 2)]
+    return [(even[i][0] + turned[i][0], even[i][1] + turned[i][1]) for i in range(order // 2)] + [
+        (even[i][0] - turned[i][0], even[i][1] - turned[i][1]) for i in range(order // 2)
+    ]
+
+
+def conv_kernel(
+    values_ref, filter_ref, tables_ref, twist_ref, out_ref,
+    got_values, got_filter, wave_high, wave_low, signal, result,
+    own_sem, send_sem, recv_sem, pass_send, pass_recv,
+):
+    device = lax.axis_index("ctx")
+    group = lax.axis_index("groups")
+    count = len(MASKS)
+    tokens = values_ref.shape[0]
+    block = values_ref.shape[1] // count
+    peers = [flip_bits(device, mask) for mask in range(count)]
+    barrier = pltpu.get_barrier_semaphore()
+    for mask in range(1, count):
+        pl.semaphore_signal(
+            barrier, inc=1, device_id={"ctx": peers[mask]}, device_id_type=pl.DeviceIdType.MESH
+        )
+    pl.semaphore_signal(
+        barrier, inc=1, device_id={"groups": 1 - group}, device_id_type=pl.DeviceIdType.MESH
+    )
+
+    def lanes(index):
+        return pl.ds(pl.multiple_of(index * block, block), block)
+
+    def to_peer(kind, mask, src, dst):
+        return pltpu.make_async_remote_copy(
+            src_ref=src,
+            dst_ref=dst,
+            send_sem=send_sem.at[kind, mask],
+            recv_sem=recv_sem.at[kind, mask],
+            device_id={"ctx": peers[mask]},
+            device_id_type=pl.DeviceIdType.MESH,
+        )
+
+    own = [
+        pltpu.make_async_copy(values_ref.at[:, lanes(device)], got_values.at[device], own_sem.at[0]),
+        pltpu.make_async_copy(
+            filter_ref.at[:, :, :, lanes(device)], got_filter.at[:, :, device], own_sem.at[1]
+        ),
+    ]
+    for copy in own:
+        copy.start()
+    pl.semaphore_wait(barrier, count)
+    issue = (15, 14, 13, 12, 11, 10, 9, 8, 7, 6, 5, 4, 3, 2, 1)
+    sent_values, sent_filter = {}, {}
+    for mask in issue:
+        sent_values[mask] = to_peer(
+            0, mask, values_ref.at[:, lanes(peers[mask])], got_values.at[device]
+        )
+        sent_values[mask].start()
+    for mask in issue:
+        sent_filter[mask] = to_peer(
+            1, mask, filter_ref.at[:, group, :, lanes(peers[mask])], got_filter.at[:, group, device]
+        )
+        sent_filter[mask].start()
+    own[0].wait()
+    for mask in issue:
+        sent_values[mask].wait()
+
+    def reverse(index):
+        return int(reverse_bits(count)[index])
+
+    half = tokens
+    tile = 16
+
+    @pl.loop(0, tokens // tile)
+    def _(step):
+        here = pl.ds(pl.multiple_of(step * tile, tile), tile)
+        there = pl.ds(pl.multiple_of(half + step * tile, tile), tile)
+        samples = [got_values[source, here, :].astype(jnp.float32) for source in range(count)]
+        zero = jnp.zeros_like(samples[0])
+        for parity in range(2):
+            pairs = [
+                times_root((item, None), -source * parity, 2 * count)
+                for source, item in enumerate(samples)
+            ]
+            pairs = [(re, zero if im is None else im) for re, im in pairs]
+            waves = short_transform(pairs, -1)
+            for place in range(count):
+                re, im = waves[reverse(place)]
+                column = 2 * place + parity
+                cos = twist_ref[here, column : column + 1]
+                sin = twist_ref[here, 2 * count + column : 2 * count + column + 1]
+                for rows, item in ((here, re * cos - im * sin), (there, re * sin + im * cos)):
+                    high = item.astype(jnp.bfloat16)
+                    columns = slice(column * block, (column + 1) * block)
+                    wave_high[rows, columns] = high
+                    wave_low[rows, columns] = (item - high.astype(jnp.float32)).astype(jnp.bfloat16)
+
+    width = 4 * block
+
+    def product(which, columns):
+        high, low = wave_high[:, columns], wave_low[:, columns]
+        return (
+            jnp.dot(tables_ref[which], high, preferred_element_type=jnp.float32)
+            + jnp.dot(tables_ref[which], low, preferred_element_type=jnp.float32)
+            + jnp.dot(tables_ref[which + 1], high, preferred_element_type=jnp.float32)
+        )
+
+    steps = 2 * count * block // width
+
+    @pl.loop(0, steps)
+    def _(step):
+        columns = pl.ds(pl.multiple_of(step * width, width), width)
+        signal[:, columns] = product(0, columns)
+
+    own[1].wait()
+    passed = {}
+    for mask in issue:
+        sent_filter[mask].wait()
+        slab = got_filter.at[:, group, peers[mask]]
+        passed[mask] = pltpu.make_async_remote_copy(
+            src_ref=slab,
+            dst_ref=slab,
+            send_sem=pass_send.at[mask],
+            recv_sem=pass_recv.at[mask],
+            device_id={"groups": 1 - group},
+            device_id_type=pl.DeviceIdType.MESH,
+        )
+        passed[mask].start()
+    for mask in issue:
+        passed[mask].wait()
+
+    @pl.loop(0, count)
+    def _(place):
+        for parity in range(2):
+            columns = pl.ds(pl.multiple_of((2 * place + parity) * block, block), block)
+            re, im = signal[0:half, columns], signal[half : 2 * half, columns]
+            filter_re = got_filter[0, parity, place].astype(jnp.float32)
+            filter_im = got_filter[1, parity, place].astype(jnp.float32)
+            for rows, item in (
+                (slice(0, half), re * filter_re - im * filter_im),
+                (slice(half, 2 * half), re * filter_im + im * filter_re),
+            ):
+                high = item.astype(jnp.bfloat16)
+                wave_high[rows, columns] = high
+                wave_low[rows, columns] = (item - high.astype(jnp.float32)).astype(jnp.bfloat16)
+
+    @pl.loop(0, steps)
+    def _(step):
+        columns = pl.ds(pl.multiple_of(step * width, width), width)
+        signal[:, columns] = product(2, columns)
+
+    scale = 1.0 / (2 * count * tokens)
+
+    @pl.loop(0, tokens // tile)
+    def _(step):
+        here = pl.ds(pl.multiple_of(step * tile, tile), tile)
+        there = pl.ds(pl.multiple_of(half + step * tile, tile), tile)
+        total = None
+        for parity in range(2):
+            waves = [None] * count
+            for place in range(count):
+                column = 2 * place + parity
+                columns = slice(column * block, (column + 1) * block)
+                re, im = signal[here, columns], signal[there, columns]
+                cos = twist_ref[here, column : column + 1]
+                sin = twist_ref[here, 2 * count + column : 2 * count + column + 1]
+                waves[reverse(place)] = (re * cos + im * sin, im * cos - re * sin)
+            pairs = short_transform(waves, 1)
+            parts = [times_root(pair, source * parity, 2 * count)[0] for source, pair in enumerate(pairs)]
+            total = parts if total is None else [left + right for left, right in zip(total, parts)]
+        for source in range(count):
+            result[source, here, :] = (total[source] * scale).astype(jnp.bfloat16)
+
+    out_ref[:, lanes(device)] = result[device]
+    returned = {}
+    for mask in issue:
+        returned[mask] = to_peer(2, mask, result.at[peers[mask]], out_ref.at[:, lanes(device)])
+        returned[mask].start()
+    for mask in issue:
+        returned[mask].wait()
+
+
+def run_convolution(value_stream, filter_spectrum):
+    tokens, channels = value_stream.shape
+    count = len(MASKS)
+    block = channels // count
+    vmem = pl.BlockSpec(memory_space=pltpu.VMEM)
+    bf16 = jnp.bfloat16
+    return pl.pallas_call(
+        conv_kernel,
+        out_shape=jax.ShapeDtypeStruct((tokens, channels), bf16),
+        in_specs=[vmem, pl.BlockSpec(memory_space=pl.ANY), vmem, vmem],
+        out_specs=vmem,
+        scratch_shapes=[
+            pltpu.VMEM((count, tokens, block), bf16),
+            pltpu.VMEM((2, 2, count, tokens, block), bf16),
+            pltpu.VMEM((2 * tokens, 2 * channels), bf16),
+            pltpu.VMEM((2 * tokens, 2 * channels), bf16),
+            pltpu.VMEM((2 * tokens, 2 * channels), jnp.float32),
+            pltpu.VMEM((count, tokens, block), bf16),
+            pltpu.SemaphoreType.DMA((2,)),
+            pltpu.SemaphoreType.DMA((3, count)),
+            pltpu.SemaphoreType.DMA((3, count)),
+            pltpu.SemaphoreType.DMA((count,)),
+            pltpu.SemaphoreType.DMA((count,)),
+        ],
+        compiler_params=pltpu.CompilerParams(
+            collective_id=2, has_side_effects=True, vmem_limit_bytes=48 * 1024 * 1024
+        ),
+    )(value_stream, filter_spectrum, inner_tables(tokens), twist_table(count, tokens))
 
 
 def expert_kernel(
@@ -288,17 +541,23 @@
     tok_rows, channels = value_stream.shape
     size_ctx = lax.axis_size("ctx")
     block = channels // size_ctx
+    expert_count = router.shape[1]
+    if (
+        size_ctx == expert_count == len(MASKS)
+        and lax.axis_size("groups") == 2
+        and block == tok_rows == 128
+        and w_gate.shape[1] % 256 == 0
+    ):
+        long_conv = run_convolution(value_stream, filter_spectrum)
+        return run_experts(
+            long_conv, gate_stream, router, w_gate, w_up, w_down, route_ids, route_slots
+        )
     arrived = lax.all_to_all(value_stream, "ctx", split_axis=1, concat_axis=0, tiled=True)
     filter_all = lax.all_to_all(filter_spectrum, "ctx", split_axis=3, concat_axis=2, tiled=True)
     long_conv = convolve(arrived, filter_all, size_ctx, tok_rows, block)
     long_conv = lax.all_to_all(
         long_conv.astype(jnp.bfloat16), "ctx", split_axis=0, concat_axis=1, tiled=True
     )
-    expert_count = router.shape[1]
-    if size_ctx == expert_count == len(MASKS) and channels % 512 == 0 and w_gate.shape[1] % 256 == 0:
-        return run_experts(
-            long_conv, gate_stream, router, w_gate, w_up, w_down, route_ids, route_slots
-        )
     long_conv = long_conv.astype(jnp.float32)
     hyena_out = (gate_stream.astype(jnp.float32) * long_conv).astype(jnp.bfloat16)
     hyena32 = hyena_out.astype(jnp.float32)

time: 202 us -> 155 us (0.77)
  Pallas kernels: 66.8 us -> 145 us
  waiting for transfers between devices: 41 us -> 0 us
  matrix products: 36.9 us -> 0 us
  local copies, waits for them, and re-layouts: 31.8 us -> 7.18 us
  starting transfers between devices: 22.7 us -> 0 us
    pallas_call x0 -> x1, Pallas kernels: none -> 78.6 us  [run_convolution(): pl.pallas_call(conv_kernel, out_shape=jax.ShapeDtypeStruct((tokens, chann...]
    all_to_all x3 -> x0, waiting for transfers between devices: 41 us -> none  [the longest x1 19 us: local(): lax.all_to_all(filter_spectrum, 'ctx', split_axis=3, concat_axis=2, tiled...]
    dot_general x4 -> x0, matrix products: 36.9 us -> none  [the longest x1 15.2 us: convolve(): spread = jnp.einsum('rqt,rqc->rtc', fine, signal, precision=highest)]
    all_to_all x3 -> x0, starting transfers between devices: 22.7 us -> none  [the longest x1 11.2 us: local(): lax.all_to_all(long_conv.astype(jnp.bfloat16), 'ctx', split_axis=0, conca...]
    reshape x2 -> x0, local copies, waits for them, and re-layouts: 9.92 us -> none  [the longest x1 4.99 us: convolve(): spread = spread.reshape(2 * rho_count, tok_rows * block)]
    unnamed x21 -> x11, local copies, waits for them, and re-layouts: 12.4 us -> 7.18 us
    convert_element_type x1 -> x0, local copies, waits for them, and re-layouts: 5.02 us -> none  [convolve(): filter_all.astype(jnp.float32).reshape(2, rho_count, tok_rows, block)]
    slice x1 -> x0, local copies, waits for them, and re-layouts: 2.64 us -> none  [convolve(): real_part = signal[:, 0] * filter32[0] - signal[:, 1] * filter32[1]]
  transfers between devices with their start and end apart: 3 -> 0, of which waited for: 3 -> 0; matrix products, arithmetic and copies ran while one was open for 14% -> 0% of each run, Pallas kernels for 0% -> 0%
where the time goes in v3:
time: 155 us
  Pallas kernels  145 us (94%)
  local copies, waits for them, and re-layouts  7.18 us (5%)
  other arithmetic  2.69 us (2%)
    pallas_call x1, Pallas kernels, run_convolution(): pl.pallas_call(conv_kernel, out_shape=jax.ShapeDtypeStruct((tokens, chann...  78.6 us
    pallas_call x1, Pallas kernels, run_experts(): pl.pallas_call(expert_kernel, out_shape=jax.ShapeDtypeStruct((tokens, cha...  66.6 us
    unnamed x11, local copies, waits for them, and re-layouts  7.18 us

profile of v3, /device:TPU:0, one launch (start us, length us, event | category | flops | bytes accessed | tf_op | source)
XLA Modules:
  0.0 155.0 jit_solution(12643363183149096006)
XLA Ops:
  0.0 0.7 broadcast_xor_fusion
  0.7 0.7 select_reduce_fusion
  1.4 1.3 and_select_fusion
  2.7 0.0 copy-start.1
  2.7 1.6 %copy-done.1 = bf16[2,2,128,2048]{3,2,1,0:T(8,128)(2,1)S(1)} copy-done((bf16[2,2,128,2048]{3,2,1,0:T(8,128)(2,1)S(1)}, bf16[2,2,128,2048]{3,2,1,0:T(8,128)(2,1)}, u32[]{:S(2)}) %copy-start.1) | copy-done | bytes 2097176
  4.3 0.0 copy-start.2
  4.3 1.0 copy-done.2
  5.3 0.0 copy-start.3
  5.3 1.0 copy-done.3
  6.4 0.0 copy-start.4
  6.4 0.8 copy-done.4
  7.2 78.6 %shard_map.118.conv_ref = bf16[128,2048]{1,0:T(8,128)(2,1)S(1)} custom-call(bf16[128,2048]{1,0:T(8,128)(2,1)S(1)} %copy-done.2, bf16[2,2,128,2048]{3,2,1,0:T(8,128)(2,1)S(1)} %copy-done.1, bf16[4,256,256]{2,1,0:T(8,128)(2,1)S(1)} %copy-done.3, f32[128,64]{1,0:T(8,128)S(1)} %copy-done.4), custom_call_target="tpu_custom_call" | custom-call | tf_op jit(solution)/shard_map/pallas_call | solution.py:307
  85.8 0.0 copy-start
  85.8 0.8 copy-done
  86.6 66.6 %shard_map.119 = bf16[128,2048]{1,0:T(8,128)(2,1)} custom-call(bf16[128,2048]{1,0:T(8,128)(2,1)} %copy-done, bf16[128,2048]{1,0:T(8,128)(2,1)} %stream_ref.1, bf16[16,2048]{1,0:T(8,128)(2,1)} %bitcast.1, s32[2,128]{1,0:T(2,128)} %ids_ref.1, s32[2,128]{1,0:T(2,128)} %get-tuple-element.6.head_ref, s32[2,128]{1,0:T(2,128)} %get-tuple-element.5.tail_ref, ...), custom_call_target="tpu_custom_call" | custom-call | tf_op jit(solution)/shard_map/pallas_call | solution.py:512
  153.1 1.9 %copy.14 = bf16[128,2048]{1,0:T(8,128)(2,1)} copy(bf16[128,2048]{1,0:T(8,128)(2,1)} %shard_map.119) | data formatting | bytes 1048576
Async XLA Ops:
  2.7 1.6 %copy-start.1 = (bf16[2,2,128,2048]{3,2,1,0:T(8,128)(2,1)S(1)}, bf16[2,2,128,2048]{3,2,1,0:T(8,128)(2,1)}, u32[]{:S(2)}) copy-start(bf16[2,2,128,2048]{3,2,1,0:T(8,128)(2,1)} %filter_ref.1) | copy-start | bytes 6291460
  4.3 1.0 copy-start.2
  5.3 1.0 copy-start.3
  6.4 0.8 copy-start.4
  85.8 0.8 copy-start

commit v4 on v3

--- a/solution.py
+++ b/solution.py
@@ -126,8 +126,8 @@
 
 
 def conv_kernel(
-    values_ref, filter_ref, tables_ref, twist_ref, out_ref,
-    got_values, got_filter, wave_high, wave_low, signal, result,
+    values_ref, filter_ref, tables_hbm, twist_hbm, out_ref,
+    tables_ref, twist_ref, got_values, got_filter, wave_high, wave_low, signal, result,
     own_sem, send_sem, recv_sem, pass_send, pass_recv,
 ):
     device = lax.axis_index("ctx")
@@ -164,24 +164,41 @@
             filter_ref.at[:, :, :, lanes(device)], got_filter.at[:, :, device], own_sem.at[1]
         ),
     ]
-    for copy in own:
-        copy.start()
+    own += [
+        pltpu.make_async_copy(tables_hbm, tables_ref, own_sem.at[2]),
+        pltpu.make_async_copy(twist_hbm, twist_ref, own_sem.at[3]),
+    ]
     pl.semaphore_wait(barrier, count)
     issue = (15, 14, 13, 12, 11, 10, 9, 8, 7, 6, 5, 4, 3, 2, 1)
-    sent_values, sent_filter = {}, {}
+    sent_values, sent_filter, passed = {}, {}, {}
+    for mask in issue:
+        sent_filter[mask] = to_peer(
+            1, mask, filter_ref.at[:, group, :, lanes(peers[mask])], got_filter.at[:, group, device]
+        )
+        sent_filter[mask].start()
     for mask in issue:
         sent_values[mask] = to_peer(
             0, mask, values_ref.at[:, lanes(peers[mask])], got_values.at[device]
         )
         sent_values[mask].start()
+    for copy in own:
+        copy.start()
     for mask in issue:
-        sent_filter[mask] = to_peer(
-            1, mask, filter_ref.at[:, group, :, lanes(peers[mask])], got_filter.at[:, group, device]
-        )
-        sent_filter[mask].start()
-    own[0].wait()
+        sent_filter[mask].wait_recv()
+        slab = got_filter.at[:, group, peers[mask]]
+        passed[mask] = pltpu.make_async_remote_copy(
+            src_ref=slab,
+            dst_ref=slab,
+            send_sem=pass_send.at[mask],
+            recv_sem=pass_recv.at[mask],
+            device_id={"groups": 1 - group},
+            device_id_type=pl.DeviceIdType.MESH,
+        )
+        passed[mask].start()
+    for copy in own:
+        copy.wait()
     for mask in issue:
-        sent_values[mask].wait()
+        sent_values[mask].wait_recv()
 
     def reverse(index):
         return int(reverse_bits(count)[index])
@@ -230,22 +247,8 @@
         columns = pl.ds(pl.multiple_of(step * width, width), width)
         signal[:, columns] = product(0, columns)
 
-    own[1].wait()
-    passed = {}
     for mask in issue:
-        sent_filter[mask].wait()
-        slab = got_filter.at[:, group, peers[mask]]
-        passed[mask] = pltpu.make_async_remote_copy(
-            src_ref=slab,
-            dst_ref=slab,
-            send_sem=pass_send.at[mask],
-            recv_sem=pass_recv.at[mask],
-            device_id={"groups": 1 - group},
-            device_id_type=pl.DeviceIdType.MESH,
-        )
-        passed[mask].start()
-    for mask in issue:
-        passed[mask].wait()
+        passed[mask].wait_recv()
 
     @pl.loop(0, count)
     def _(place):
@@ -296,6 +299,9 @@
         returned[mask].start()
     for mask in issue:
         returned[mask].wait()
+        passed[mask].wait_send()
+        sent_values[mask].wait_send()
+        sent_filter[mask].wait_send()
 
 
 def run_convolution(value_stream, filter_spectrum):
@@ -307,16 +313,18 @@
     return pl.pallas_call(
         conv_kernel,
         out_shape=jax.ShapeDtypeStruct((tokens, channels), bf16),
-        in_specs=[vmem, pl.BlockSpec(memory_space=pl.ANY), vmem, vmem],
+        in_specs=[pl.BlockSpec(memory_space=pl.ANY)] * 4,
         out_specs=vmem,
         scratch_shapes=[
+            pltpu.VMEM((4, 2 * tokens, 2 * tokens), bf16),
+            pltpu.VMEM((tokens, 4 * count), jnp.float32),
             pltpu.VMEM((count, tokens, block), bf16),
             pltpu.VMEM((2, 2, count, tokens, block), bf16),
             pltpu.VMEM((2 * tokens, 2 * channels), bf16),
             pltpu.VMEM((2 * tokens, 2 * channels), bf16),
             pltpu.VMEM((2 * tokens, 2 * channels), jnp.float32),
             pltpu.VMEM((count, tokens, block), bf16),
-            pltpu.SemaphoreType.DMA((2,)),
+            pltpu.SemaphoreType.DMA((4,)),
             pltpu.SemaphoreType.DMA((3, count)),
             pltpu.SemaphoreType.DMA((3, count)),
             pltpu.SemaphoreType.DMA((count,)),
@@ -329,8 +337,8 @@
 
 
 def expert_kernel(
-    conv_ref, stream_ref, router_ref, ids_ref, head_ref, tail_ref, wg_hbm, wu_hbm, wd_hbm, out_ref,
-    hyena, send_head, send_tail, recv_head, recv_tail, done_head, done_tail, back_head, back_tail,
+    conv_ref, stream_hbm, router_ref, ids_ref, slots_ref, wg_hbm, wu_hbm, wd_hbm, out_ref,
+    stream_ref, hyena, send_head, send_tail, recv_head, recv_tail, done_head, done_tail, back_head, back_tail,
     rows, hidden, wg, wu, wd, tail_sum, gates, own_sem, send_sem, recv_sem, weight_sem,
 ):
     device = lax.axis_index("ctx")
@@ -344,13 +352,23 @@
         pltpu.make_async_copy(src, dst, weight_sem.at[i])
         for i, (src, dst) in enumerate(((wg_hbm, wg), (wu_hbm, wu), (wd_hbm, wd)))
     ]
-    for copy in weights:
-        copy.start()
+    stream_copy = pltpu.make_async_copy(stream_hbm, stream_ref, weight_sem.at[3])
+    stream_copy.start()
     barrier = pltpu.get_barrier_semaphore()
     for slot in range(1, count):
         pl.semaphore_signal(
             barrier, inc=1, device_id={"ctx": peers[slot]}, device_id_type=pl.DeviceIdType.MESH
         )
+    for copy in weights:
+        copy.start()
+    ids = ids_ref[...]
+    picks = slots_ref[...]
+    position = jnp.zeros_like(ids)
+    for slot in range(count):
+        position = jnp.where(ids == peers[slot], slot, position)
+    head = jnp.where(picks < HEAD, position * HEAD + picks, -1024)
+    tail = jnp.where((picks >= HEAD) & (picks < CAP), position * HEAD + picks - HEAD, -1024)
+    stream_copy.wait()
     mixed = (stream_ref[...].astype(jnp.float32) * conv_ref[...].astype(jnp.float32)).astype(jnp.bfloat16)
     hyena[...] = mixed
     mixed32 = mixed.astype(jnp.float32)
@@ -365,8 +383,6 @@
         first, second = hits(targets, shift)
         return jnp.where(first | second, 1.0, 0.0).astype(jnp.bfloat16)
 
-    head = head_ref[...]
-    tail = tail_ref[...]
     send_head[...] = jnp.dot(one_hot(head, 0), normed, preferred_element_type=jnp.float32).astype(jnp.bfloat16)
     packed = jnp.zeros((slots, quarter), jnp.float32)
     for part in range(QUARTERS):
@@ -412,7 +428,6 @@
         router_ref[...], normed, (((1,), (1,)), ((), ())), preferred_element_type=jnp.float32
     )
     expert_row = lax.broadcasted_iota(jnp.int32, logits.shape, 0)
-    ids = ids_ref[...]
     for pick in range(2):
         chosen = jnp.sum(
             jnp.where(expert_row == ids[pick : pick + 1, :], logits, 0.0), axis=0, keepdims=True
@@ -496,25 +511,15 @@
     slots = count * HEAD
     half_rows = slots // 2 + (count // 2) * TAIL
     quarter = channels // QUARTERS
-    device = lax.axis_index("ctx")
-    place = jnp.asarray(np.argsort(np.asarray(MASKS)), jnp.int32)
-    offset = jnp.bitwise_xor(route_ids, device)
-    position = jnp.sum(
-        jnp.where(offset[:, :, None] == jnp.arange(count)[None, None, :], place[None, None, :], 0), axis=2
-    )
-    head = jnp.where(route_slots < HEAD, position * HEAD + route_slots, -1024)
-    tail = jnp.where(
-        (route_slots >= HEAD) & (route_slots < CAP), position * HEAD + route_slots - HEAD, -1024
-    )
     vmem = pl.BlockSpec(memory_space=pltpu.VMEM)
     hbm = pl.BlockSpec(memory_space=pl.ANY)
     bf16 = jnp.bfloat16
     return pl.pallas_call(
         expert_kernel,
         out_shape=jax.ShapeDtypeStruct((tokens, channels), bf16),
-        in_specs=[vmem] * 6 + [hbm] * 3,
+        in_specs=[vmem, hbm, vmem, vmem, vmem] + [hbm] * 3,
         out_specs=vmem,
-        scratch_shapes=[pltpu.VMEM((tokens, channels), bf16)]
+        scratch_shapes=[pltpu.VMEM((tokens, channels), bf16)] * 2
         + [pltpu.VMEM((slots, channels), bf16), pltpu.VMEM((slots, quarter), bf16)] * 4
         + [
             pltpu.VMEM((half_rows, channels), bf16),
@@ -527,12 +532,12 @@
             pltpu.SemaphoreType.DMA((2, 2)),
             pltpu.SemaphoreType.DMA((2, 2, count)),
             pltpu.SemaphoreType.DMA((2, 2, count)),
-            pltpu.SemaphoreType.DMA((3,)),
+            pltpu.SemaphoreType.DMA((4,)),
         ],
         compiler_params=pltpu.CompilerParams(
             collective_id=1, has_side_effects=True, vmem_limit_bytes=56 * 1024 * 1024
         ),
-    )(long_conv, gate_stream, router.T, route_ids, head, tail, w_gate, w_up, w_down)
+    )(long_conv, gate_stream, router.T, route_ids, route_slots, w_gate, w_up, w_down)
 
 
 def local(

time: 155 us -> 145 us (0.935)
  Pallas kernels: 145 us -> 137 us
  other arithmetic: 2.69 us -> 0 us
    pallas_call x1, Pallas kernels: 78.6 us -> 67 us  [run_convolution(): pl.pallas_call(conv_kernel, out_shape=jax.ShapeDtypeStruct((tokens, chann...]
    pallas_call x1, Pallas kernels: 66.6 us -> 70.2 us  [run_experts(): pl.pallas_call(expert_kernel, out_shape=jax.ShapeDtypeStruct((tokens, cha...]
where the time goes in v4:
time: 145 us
  Pallas kernels  137 us (94%)
  local copies, waits for them, and re-layouts  7.18 us (5%)
    pallas_call x1, Pallas kernels, run_experts(): pl.pallas_call(expert_kernel, out_shape=jax.ShapeDtypeStruct((tokens, cha...  70.2 us
    pallas_call x1, Pallas kernels, run_convolution(): pl.pallas_call(conv_kernel, out_shape=jax.ShapeDtypeStruct((tokens, chann...  67 us
    unnamed x11, local copies, waits for them, and re-layouts  7.18 us

profile of v4, /device:TPU:0, one launch (start us, length us, event | category | flops | bytes accessed | tf_op | source)
XLA Modules:
  0.0 144.5 jit_solution(1253389667818617750)
XLA Ops:
  0.0 0.0 copy-start.1
  0.0 1.6 %copy-done.1 = bf16[2,2,128,2048]{3,2,1,0:T(8,128)(2,1)S(1)} copy-done((bf16[2,2,128,2048]{3,2,1,0:T(8,128)(2,1)S(1)}, bf16[2,2,128,2048]{3,2,1,0:T(8,128)(2,1)}, u32[]{:S(2)}) %copy-start.1) | copy-done | bytes 2097176
  1.6 0.0 copy-start.2
  1.6 1.0 copy-done.2
  2.6 0.0 copy-start.3
  2.6 1.0 copy-done.3
  3.7 0.0 copy-start.4
  3.7 0.8 copy-done.4
  4.5 67.0 %shard_map.109.conv_ref = bf16[128,2048]{1,0:T(8,128)(2,1)S(1)} custom-call(bf16[128,2048]{1,0:T(8,128)(2,1)S(1)} %copy-done.2, bf16[2,2,128,2048]{3,2,1,0:T(8,128)(2,1)S(1)} %copy-done.1, bf16[4,256,256]{2,1,0:T(8,128)(2,1)S(1)} %copy-done.3, f32[128,64]{1,0:T(8,128)S(1)} %copy-done.4), custom_call_target="tpu_custom_call" | custom-call | tf_op jit(solution)/shard_map/pallas_call | solution.py:313
  71.6 0.0 copy-start
  71.6 0.8 copy-done
  72.4 70.2 %shard_map.110 = bf16[128,2048]{1,0:T(8,128)(2,1)} custom-call(bf16[128,2048]{1,0:T(8,128)(2,1)} %copy-done, bf16[128,2048]{1,0:T(8,128)(2,1)} %stream_hbm.1, bf16[16,2048]{1,0:T(8,128)(2,1)} %bitcast.1, s32[2,128]{1,0:T(2,128)} %ids_ref.1, s32[2,128]{1,0:T(2,128)} %slots_ref.1, bf16[2048,2816]{1,0:T(8,128)(2,1)} %wg_hbm.1, bf16[2048,2816]{1,0:T(8,128)(2,1)} %wu_hbm.1, ...), custom_call_target="tpu_custom_call" | custom-call | tf_op jit(solution)/shard_map/pallas_call | solution.py:517
  142.6 1.9 %copy.13 = bf16[128,2048]{1,0:T(8,128)(2,1)} copy(bf16[128,2048]{1,0:T(8,128)(2,1)} %shard_map.110) | data formatting | bytes 1048576
Async XLA Ops:
  0.0 1.6 %copy-start.1 = (bf16[2,2,128,2048]{3,2,1,0:T(8,128)(2,1)S(1)}, bf16[2,2,128,2048]{3,2,1,0:T(8,128)(2,1)}, u32[]{:S(2)}) copy-start(bf16[2,2,128,2048]{3,2,1,0:T(8,128)(2,1)} %filter_ref.1) | copy-start | bytes 6291460
  1.6 1.0 copy-start.2
  2.6 1.0 copy-start.3
  3.7 0.8 copy-start.4
  71.6 0.8 copy-start

commit v5 on v4

--- a/solution.py
+++ b/solution.py
@@ -169,7 +169,7 @@
         pltpu.make_async_copy(twist_hbm, twist_ref, own_sem.at[3]),
     ]
     pl.semaphore_wait(barrier, count)
-    issue = (15, 14, 13, 12, 11, 10, 9, 8, 7, 6, 5, 4, 3, 2, 1)
+    issue = (15, 7, 14, 6, 13, 5, 12, 4, 11, 3, 10, 2, 9, 1, 8)
     sent_values, sent_filter, passed = {}, {}, {}
     for mask in issue:
         sent_filter[mask] = to_peer(
@@ -331,7 +331,7 @@
             pltpu.SemaphoreType.DMA((count,)),
         ],
         compiler_params=pltpu.CompilerParams(
-            collective_id=2, has_side_effects=True, vmem_limit_bytes=48 * 1024 * 1024
+            collective_id=2, has_side_effects=True, vmem_limit_bytes=61 * 1024 * 1024
         ),
     )(value_stream, filter_spectrum, inner_tables(tokens), twist_table(count, tokens))
 
@@ -418,7 +418,7 @@
         return copies
 
     half = count // 2
-    issue = (7, 6, 5, 4, 3, 2, 1, 0, 15, 14, 13, 12, 11, 10, 9, 8)
+    issue = (7, 3, 6, 2, 5, 1, 4, 0, 15, 11, 14, 10, 13, 9, 12, 8)
     outward = {slot: exchange(slot, 0) for slot in range(count)}
     inward = {slot: exchange(slot, 1) for slot in range(count)}
     for slot in issue:
@@ -483,25 +483,26 @@
             for copy in inward[slot]:
                 copy.start()
 
-    def weighted(targets, shift, values):
+    def weights_of(targets, shift):
         first, second = hits(targets, shift)
         mix = jnp.where(first, gates[0:1, :], 0.0) + jnp.where(second, gates[1:2, :], 0.0)
         high = mix.astype(jnp.bfloat16)
-        low = (mix - high.astype(jnp.float32)).astype(jnp.bfloat16)
+        return high, (mix - high.astype(jnp.float32)).astype(jnp.bfloat16)
+
+    def weighted(pair, values):
         dims = (((0,), (0,)), ((), ()))
-        return lax.dot_general(high, values, dims, preferred_element_type=jnp.float32) + lax.dot_general(
-            low, values, dims, preferred_element_type=jnp.float32
-        )
-
+        return sum(
+            lax.dot_general(piece, values, dims, preferred_element_type=jnp.float32) for piece in pair
+        )
+
+    head_pair = weights_of(head, 0)
+    tail_pairs = [weights_of(tail, TAIL * part) for part in range(QUARTERS)]
     for slot in range(count):
         for copy in inward[slot]:
             copy.wait()
-    for part in range(QUARTERS):
-        columns = slice(part * quarter, (part + 1) * quarter)
-        total = hyena[:, columns].astype(jnp.float32)
-        total = total + weighted(head, 0, back_head[:, columns])
-        total = total + weighted(tail, TAIL * part, back_tail[...])
-        out_ref[:, columns] = total.astype(jnp.bfloat16)
+    out_ref[...] = (hyena[...].astype(jnp.float32) + weighted(head_pair, back_head[...]) + jnp.concatenate(
+        [weighted(pair, back_tail[...]) for pair in tail_pairs], axis=1
+    )).astype(jnp.bfloat16)
 
 
 def run_experts(long_conv, gate_stream, router, w_gate, w_up, w_down, route_ids, route_slots):

time: 145 us -> 133 us (0.917)
  Pallas kernels: 137 us -> 131 us
  local copies, waits for them, and re-layouts: 7.18 us -> 1.88 us
    unnamed x11 -> x1, local copies, waits for them, and re-layouts: 7.18 us -> 1.88 us
    pallas_call x1, Pallas kernels: 70.2 us -> 65.9 us  [run_experts(): pl.pallas_call(expert_kernel, out_shape=jax.ShapeDtypeStruct((tokens, cha...]
    pallas_call x1, Pallas kernels: 67 us -> 65 us  [run_convolution(): pl.pallas_call(conv_kernel, out_shape=jax.ShapeDtypeStruct((tokens, chann...]
where the time goes in v5:
time: 133 us
  Pallas kernels  131 us (98%)
  local copies, waits for them, and re-layouts  1.88 us (1%)
    pallas_call x1, Pallas kernels, run_experts(): pl.pallas_call(expert_kernel, out_shape=jax.ShapeDtypeStruct((tokens, cha...  65.9 us
    pallas_call x1, Pallas kernels, run_convolution(): pl.pallas_call(conv_kernel, out_shape=jax.ShapeDtypeStruct((tokens, chann...  65 us

profile of v5, /device:TPU:0, one launch (start us, length us, event | category | flops | bytes accessed | tf_op | source)
XLA Modules:
  0.0 132.8 jit_solution(15769879333591913253)
XLA Ops:
  0.0 65.0 %shard_map.109.conv_ref = bf16[128,2048]{1,0:T(8,128)(2,1)} custom-call(bf16[128,2048]{1,0:T(8,128)(2,1)} %values_ref.1, bf16[2,2,128,2048]{3,2,1,0:T(8,128)(2,1)} %filter_ref.1, bf16[4,256,256]{2,1,0:T(8,128)(2,1)} %constant.4.clone.tables_hbm, f32[128,64]{1,0:T(8,128)} %constant.5.clone.twist_hbm), custom_call_target="tpu_custom_call" | custom-call | tf_op jit(solution)/shard_map/pallas_call | solution.py:313
  65.0 65.9 %shard_map.110 = bf16[128,2048]{1,0:T(8,128)(2,1)} custom-call(bf16[128,2048]{1,0:T(8,128)(2,1)} %shard_map.109.conv_ref, bf16[128,2048]{1,0:T(8,128)(2,1)} %stream_hbm.1, bf16[16,2048]{1,0:T(8,128)(2,1)} %bitcast.1, s32[2,128]{1,0:T(2,128)} %ids_ref.1, s32[2,128]{1,0:T(2,128)} %slots_ref.1, bf16[2048,2816]{1,0:T(8,128)(2,1)} %wg_hbm.1, ...), custom_call_target="tpu_custom_call" | custom-call | tf_op jit(solution)/shard_map/pallas_call | solution.py:518
  131.0 1.9 %copy.13 = bf16[128,2048]{1,0:T(8,128)(2,1)} copy(bf16[128,2048]{1,0:T(8,128)(2,1)} %shard_map.110) | data formatting | bytes 1048576

commit v6 on v5

--- a/solution.py
+++ b/solution.py
@@ -272,8 +272,7 @@
 
     scale = 1.0 / (2 * count * tokens)
 
-    @pl.loop(0, tokens // tile)
-    def _(step):
+    def finish(step):
         here = pl.ds(pl.multiple_of(step * tile, tile), tile)
         there = pl.ds(pl.multiple_of(half + step * tile, tile), tile)
         total = None
@@ -292,13 +291,20 @@
         for source in range(count):
             result[source, here, :] = (total[source] * scale).astype(jnp.bfloat16)
 
+    returned = []
+    for part in range(2):
+        pl.loop(part * tokens // tile // 2, (part + 1) * tokens // tile // 2)(finish)
+        span = pl.ds(part * tokens // 2, tokens // 2)
+        for mask in issue:
+            copy = to_peer(
+                2 + part, mask, result.at[peers[mask], span], out_ref.at[span, lanes(device)]
+            )
+            copy.start()
+            returned.append(copy)
     out_ref[:, lanes(device)] = result[device]
-    returned = {}
+    for copy in returned:
+        copy.wait()
     for mask in issue:
-        returned[mask] = to_peer(2, mask, result.at[peers[mask]], out_ref.at[:, lanes(device)])
-        returned[mask].start()
-    for mask in issue:
-        returned[mask].wait()
         passed[mask].wait_send()
         sent_values[mask].wait_send()
         sent_filter[mask].wait_send()
@@ -325,8 +331,8 @@
             pltpu.VMEM((2 * tokens, 2 * channels), jnp.float32),
             pltpu.VMEM((count, tokens, block), bf16),
             pltpu.SemaphoreType.DMA((4,)),
-            pltpu.SemaphoreType.DMA((3, count)),
-            pltpu.SemaphoreType.DMA((3, count)),
+            pltpu.SemaphoreType.DMA((4, count)),
+            pltpu.SemaphoreType.DMA((4, count)),
             pltpu.SemaphoreType.DMA((count,)),
             pltpu.SemaphoreType.DMA((count,)),
         ],

time: 133 us -> 131 us (0.985)
  Pallas kernels: 131 us -> 129 us
    pallas_call x1, Pallas kernels: 65.9 us -> 64 us  [run_experts(): pl.pallas_call(expert_kernel, out_shape=jax.ShapeDtypeStruct((tokens, cha...]
where the time goes in v6:
time: 131 us
  Pallas kernels  129 us (98%)
  local copies, waits for them, and re-layouts  1.88 us (1%)
    pallas_call x1, Pallas kernels, run_convolution(): pl.pallas_call(conv_kernel, out_shape=jax.ShapeDtypeStruct((tokens, chann...  65.4 us
    pallas_call x1, Pallas kernels, run_experts(): pl.pallas_call(expert_kernel, out_shape=jax.ShapeDtypeStruct((tokens, cha...  64 us

profile of v6, /device:TPU:0, one launch (start us, length us, event | category | flops | bytes accessed | tf_op | source)
XLA Modules:
  0.0 131.3 jit_solution(6696202072570184792)
XLA Ops:
  0.0 65.4 %shard_map.109.conv_ref = bf16[128,2048]{1,0:T(8,128)(2,1)} custom-call(bf16[128,2048]{1,0:T(8,128)(2,1)} %values_ref.1, bf16[2,2,128,2048]{3,2,1,0:T(8,128)(2,1)} %filter_ref.1, bf16[4,256,256]{2,1,0:T(8,128)(2,1)} %constant.4.clone.tables_hbm, f32[128,64]{1,0:T(8,128)} %constant.5.clone.twist_hbm), custom_call_target="tpu_custom_call" | custom-call | tf_op jit(solution)/shard_map/pallas_call | solution.py:319
  65.4 64.0 %shard_map.110 = bf16[128,2048]{1,0:T(8,128)(2,1)} custom-call(bf16[128,2048]{1,0:T(8,128)(2,1)} %shard_map.109.conv_ref, bf16[128,2048]{1,0:T(8,128)(2,1)} %stream_hbm.1, bf16[16,2048]{1,0:T(8,128)(2,1)} %bitcast.1, s32[2,128]{1,0:T(2,128)} %ids_ref.1, s32[2,128]{1,0:T(2,128)} %slots_ref.1, bf16[2048,2816]{1,0:T(8,128)(2,1)} %wg_hbm.1, ...), custom_call_target="tpu_custom_call" | custom-call | tf_op jit(solution)/shard_map/pallas_call | solution.py:524
  129.4 1.9 %copy.13 = bf16[128,2048]{1,0:T(8,128)(2,1)} copy(bf16[128,2048]{1,0:T(8,128)(2,1)} %shard_map.110) | data formatting | bytes 1048576
